TPU v7x, 128 devices: a whole 4x4x4 slice. The times are simulated.
128 devices in a mesh: dp: 8 (over z_hi, y), seq: 16 (over x, z_lo, core).
Axes of the slice: x: 4, y: 4, z: 4 (z_hi: 2, z_lo: 2; z = z_hi * 2 + z_lo), core: 2. Of those that a mesh axis runs over, the one named last changes fastest.
Arguments:
- sequence: bfloat16 [8, 8192, 384], P('dp', 'seq'), may hold values from -200 to 200
- conv_weight: bfloat16 [2, 3, 384, 384], replicated, may hold values from -0.1875 to 0.1875
- batch_norm_gains: float32 [3, 384], replicated, may hold values from 0.25 to 1.75
- batch_norm_shifts: float32 [3, 384], replicated, may hold values from -0.5 to 0.5
- head_weight: bfloat16 [384, 5313], replicated, may hold values from -0.3125 to 0.3125
- head_bias: float32 [5313], replicated, may hold values from -1 to 1
- targets: int32 [8, 8192, 5313], P('dp', 'seq'), may hold values from 0 to 31
Outputs:
- grad_input: float32 [8, 8192, 384], P('dp', 'seq')
- grad_conv: float32 [2, 3, 384, 384], replicated
- grad_gain: float32 [3, 384], replicated
- grad_shift: float32 [3, 384], replicated
- grad_head: float32 [384, 5313], P('seq')
- grad_head_bias: float32 [5313], replicated
All inputs are finite; a program needn't handle non-finite values.
Results may differ from a plain program's by a relative error of at most 0.0057.
Values may be sent and summed in bfloat16 or wider, within the bound.
A program may use at most 128 MiB of HBM per device.

v0:
```python
import math

import jax
import jax.numpy as jnp
from jax import lax
from jax.sharding import Mesh
from jax.sharding import PartitionSpec as P

SEQ = ("seq_0", "seq_1", "seq_2")
DP = ("dp_0", "dp_1")
DP_SEQ = ("dp_0", "dp_1", "seq_0", "seq_1", "seq_2")


EPS = 1e-05


def from_behind(block, axis, distance):
    devices = range(lax.axis_size(axis))
    route = [(i - distance, i) for i in devices if i - distance in devices]
    return lax.ppermute(block, axis, route)


def one_axis_at_a_time(array, axes):
    for axis in axes:
        array = lax.psum(array, axis)
    return array


def in_one(arrays, axis):
    ends = [0]
    for a in arrays:
        ends.append(ends[-1] + a.size)
    subtotal = lax.psum(jnp.concatenate([a.ravel() for a in arrays]), axis)
    return tuple((subtotal[b:e].reshape(a.shape) for a, b, e in zip(arrays, ends, ends[1:])))


def exact_gelu_fn(value):
    return jax.nn.gelu(value, approximate=False)


def project(block, weight):
    flat = block.reshape(-1, block.shape[-1])
    return jnp.dot(flat, weight, preferred_element_type=jnp.float32).reshape(
        block.shape[:-1] + (weight.shape[-1],)
    )


def contract(left, right):
    return lax.dot_general(
        left.reshape(-1, left.shape[-1]),
        right.reshape(-1, right.shape[-1]),
        (((0,), (0,)), ((), ())),
        preferred_element_type=jnp.float32,
    )


def neighbours(block, span):
    lower_neighbour = from_behind(block, SEQ, span)
    upper_neighbour = from_behind(block, SEQ, -span)
    return (lower_neighbour, upper_neighbour)


def gelu_back(preactivation, upstream):
    return jax.vjp(exact_gelu_fn, preactivation)[1](upstream)[0]


def on_device(
    sequence, conv_weight, batch_norm_gains, batch_norm_shifts, head_weight, head_bias, targets
):
    loci_here, bins_here, width = sequence.shape
    tracks = head_weight.shape[1]
    element_count = loci_here * bins_here * lax.axis_size(DP) * lax.axis_size(SEQ)
    spans = (lax.axis_size(SEQ) // 4, lax.axis_size(SEQ) // 2)

    def batch_norm_forward(residual_field, layer_index):
        batch_mean = (
            one_axis_at_a_time(jnp.sum(residual_field, axis=(0, 1)), DP_SEQ) / element_count
        )
        centered_input = residual_field - batch_mean
        var = (
            one_axis_at_a_time(jnp.sum(centered_input * centered_input, axis=(0, 1)), DP_SEQ)
            / element_count
        )
        inverse_deviation = lax.rsqrt(var + EPS)
        normalized_input = (residual_field - batch_mean) * inverse_deviation
        preactivation = (
            normalized_input * batch_norm_gains[layer_index] + batch_norm_shifts[layer_index]
        )
        return (
            exact_gelu_fn(preactivation).astype(jnp.bfloat16),
            preactivation,
            normalized_input,
            inverse_deviation,
        )

    residual_field = sequence.astype(jnp.float32)
    saved_tensors = []
    for layer_number in range(2):
        activation_out, preactivation, normalized_input, inverse_deviation = batch_norm_forward(
            residual_field, layer_number
        )
        lower_neighbour, upper_neighbour = neighbours(activation_out, spans[layer_number])
        update = (
            project(lower_neighbour, conv_weight[layer_number, 0])
            + project(activation_out, conv_weight[layer_number, 1])
            + project(upper_neighbour, conv_weight[layer_number, 2])
        )
        saved_tensors.append(
            (
                activation_out,
                lower_neighbour,
                upper_neighbour,
                preactivation,
                normalized_input,
                inverse_deviation,
            )
        )
        residual_field = residual_field + update
    hidden_state, final_preactivation, final_normalized, final_inverse_deviation = (
        batch_norm_forward(residual_field, 2)
    )
    scale = 1.0 / math.sqrt(element_count)
    rows = hidden_state.reshape(-1, width)
    counts = targets.reshape(-1, tracks)
    logits = jnp.dot(rows, head_weight, preferred_element_type=jnp.float32) + head_bias
    dlogit = ((jnp.exp(logits) - counts.astype(jnp.float32)) * scale).astype(jnp.bfloat16)
    partial_rows = lax.psum_scatter(
        lax.dot_general(
            rows, dlogit, (((0,), (0,)), ((), ())), preferred_element_type=jnp.float32
        ).astype(jnp.bfloat16),
        SEQ,
        scatter_dimension=0,
        tiled=True,
    ).astype(jnp.float32)
    grad_head = lax.psum(partial_rows, DP)
    dhidden = lax.dot_general(
        dlogit, head_weight, (((1,), (1,)), ((), ())), preferred_element_type=jnp.float32
    )
    preact_gradient = gelu_back(final_preactivation, dhidden.reshape(loci_here, bins_here, width))
    local_bias_part = jnp.sum(dlogit.astype(jnp.float32), axis=0)
    grad_head_bias, last_shift, last_gain = lax.psum(
        (
            local_bias_part,
            jnp.sum(preact_gradient, axis=(0, 1)),
            jnp.sum(preact_gradient * final_normalized, axis=(0, 1)),
        ),
        DP_SEQ,
    )
    field_grad_input = (
        batch_norm_gains[2]
        * final_inverse_deviation
        * (
            preact_gradient
            - last_shift / element_count
            - final_normalized * last_gain / element_count
        )
    )
    gain_list = [None, None, last_gain]
    shift_list = [None, None, last_shift]
    conv_grads = [None, None]
    for layer_number in (1, 0):
        (
            activation_out,
            lower_neighbour,
            upper_neighbour,
            preactivation,
            normalized_input,
            inverse_deviation,
        ) = saved_tensors[layer_number]
        grad_low = field_grad_input.astype(jnp.bfloat16)
        below, above = neighbours(grad_low, spans[layer_number])
        dact = (
            project(above, conv_weight[layer_number, 0].T)
            + project(grad_low, conv_weight[layer_number, 1].T)
            + project(below, conv_weight[layer_number, 2].T)
        )
        local_conv = jnp.stack(
            [
                contract(lower_neighbour, grad_low),
                contract(activation_out, grad_low),
                contract(upper_neighbour, grad_low),
            ]
        )
        conv_grads[layer_number] = lax.psum(local_conv, DP_SEQ)
        preact_gradient = gelu_back(preactivation, dact)
        shift_gradient_sum, gain_gradient_sum = in_one(
            (
                jnp.sum(preact_gradient, axis=(0, 1)),
                jnp.sum(preact_gradient * normalized_input, axis=(0, 1)),
            ),
            DP_SEQ,
        )
        gain_list[layer_number] = gain_gradient_sum
        shift_list[layer_number] = shift_gradient_sum
        field_grad_input = field_grad_input + batch_norm_gains[layer_number] * inverse_deviation * (
            preact_gradient
            - shift_gradient_sum / element_count
            - normalized_input * gain_gradient_sum / element_count
        )
    grad_conv = jnp.stack(conv_grads)
    return (
        field_grad_input,
        grad_conv,
        jnp.stack(gain_list),
        jnp.stack(shift_list),
        grad_head,
        grad_head_bias,
    )


def solution(mesh):
    split = Mesh(mesh.devices.reshape(2, 4, 4, 2, 2), ("dp_0", "dp_1", "seq_0", "seq_1", "seq_2"))
    placed = (P(DP, SEQ, None), P(), P(), P(), P(), P(), P(DP, SEQ, None))
    return jax.shard_map(
        on_device,
        mesh=split,
        in_specs=placed,
        out_specs=(P(DP, SEQ, None), P(), P(), P(), P(SEQ, None), P()),
        check_vma=False,
    )
```

profile of v0, /device:TPU:0, one launch (start us, length us, event | category | flops | bytes accessed | tf_op | source)
XLA Modules:
  0.0 639.0 jit_solution(11833157485126600714)
XLA Ops:
  9.3 6.9 %psum.266 = f32[384]{0:T(512)S(1)} all-reduce(f32[384]{0:T(512)S(1)} %convert_reduce_fusion.1), channel_id=1, replica_groups=mesh['dp_0'=2,'dp_1'=4,'seq_0'=4,'seq_1'=2,'seq_2'=2] {'dp_0'}, use_global_device_ids=true, to_apply=%region_1.0 | all-reduce | flops 384 | bytes 3072 | tf_op jit(solution)/shard_map/psum | solution.py:25
  16.2 10.7 %psum.267 = f32[384]{0:T(512)S(1)} all-reduce(f32[384]{0:T(512)S(1)} %psum.266), channel_id=1, replica_groups=mesh['dp_0'=2,'dp_1'=4,'seq_0'=4,'seq_1'=2,'seq_2'=2] {'dp_1'}, use_global_device_ids=true, to_apply=%region_2.0 | all-reduce | flops 384 | bytes 3072 | tf_op jit(solution)/shard_map/psum | solution.py:25
  26.9 10.5 %psum.268 = f32[384]{0:T(512)S(1)} all-reduce(f32[384]{0:T(512)S(1)} %psum.267), channel_id=1, replica_groups=mesh['dp_0'=2,'dp_1'=4,'seq_0'=4,'seq_1'=2,'seq_2'=2] {'seq_0'}, use_global_device_ids=true, to_apply=%region_3.0 | all-reduce | flops 384 | bytes 3072 | tf_op jit(solution)/shard_map/psum | solution.py:25
  52.3 7.7 %psum.272 = f32[384]{0:T(512)S(1)} all-reduce(f32[384]{0:T(512)S(1)} %psum.271), channel_id=1, replica_groups=mesh['dp_0'=2,'dp_1'=4,'seq_0'=4,'seq_1'=2,'seq_2'=2] {'dp_1'}, use_global_device_ids=true, to_apply=%region_8.0 | all-reduce | flops 384 | bytes 3072 | tf_op jit(solution)/shard_map/psum | solution.py:25
  60.0 7.7 %psum.273 = f32[384]{0:T(512)S(1)} all-reduce(f32[384]{0:T(512)S(1)} %psum.272), channel_id=1, replica_groups=mesh['dp_0'=2,'dp_1'=4,'seq_0'=4,'seq_1'=2,'seq_2'=2] {'seq_0'}, use_global_device_ids=true, to_apply=%region_9.0 | all-reduce | flops 384 | bytes 3072 | tf_op jit(solution)/shard_map/psum | solution.py:25
  86.7 7.1 %collective-permute-done.1 = bf16[1,512,384]{2,1,0:T(8,128)(2,1)S(1)} collective-permute-done((bf16[1,512,384]{2,1,0:T(8,128)(2,1)S(1)}, bf16[1,512,384]{2,1,0:T(8,128)(2,1)S(1)}, u32[]{:S(2)}, u32[]{:S(2)}) %collective-permute-start.1) | collective-permute-done | bytes 393248 | tf_op jit(solution)/shard_map/ppermute | solution.py:20
  102.2 9.7 %psum.277 = f32[384]{0:T(512)S(1)} all-reduce(f32[384]{0:T(512)S(1)} %psum.276), channel_id=1, replica_groups=mesh['dp_0'=2,'dp_1'=4,'seq_0'=4,'seq_1'=2,'seq_2'=2] {'dp_1'}, use_global_device_ids=true, to_apply=%region_14.0 | all-reduce | flops 384 | bytes 3072 | tf_op jit(solution)/shard_map/psum | solution.py:25
  111.9 10.8 %psum.278 = f32[384]{0:T(512)S(1)} all-reduce(f32[384]{0:T(512)S(1)} %psum.277), channel_id=1, replica_groups=mesh['dp_0'=2,'dp_1'=4,'seq_0'=4,'seq_1'=2,'seq_2'=2] {'seq_0'}, use_global_device_ids=true, to_apply=%region_15.0 | all-reduce | flops 384 | bytes 3072 | tf_op jit(solution)/shard_map/psum | solution.py:25
  136.6 7.7 %psum.282 = f32[384]{0:T(512)S(1)} all-reduce(f32[384]{0:T(512)S(1)} %psum.281), channel_id=1, replica_groups=mesh['dp_0'=2,'dp_1'=4,'seq_0'=4,'seq_1'=2,'seq_2'=2] {'dp_1'}, use_global_device_ids=true, to_apply=%region_20.0 | all-reduce | flops 384 | bytes 3072 | tf_op jit(solution)/shard_map/psum | solution.py:25
  144.3 8.2 %psum.283 = f32[384]{0:T(512)S(1)} all-reduce(f32[384]{0:T(512)S(1)} %psum.282), channel_id=1, replica_groups=mesh['dp_0'=2,'dp_1'=4,'seq_0'=4,'seq_1'=2,'seq_2'=2] {'seq_0'}, use_global_device_ids=true, to_apply=%region_21.0 | all-reduce | flops 384 | bytes 3072 | tf_op jit(solution)/shard_map/psum | solution.py:25
  171.0 6.8 %collective-permute-done.3 = bf16[1,512,384]{2,1,0:T(8,128)(2,1)S(1)} collective-permute-done((bf16[1,512,384]{2,1,0:T(8,128)(2,1)S(1)}, bf16[1,512,384]{2,1,0:T(8,128)(2,1)S(1)}, u32[]{:S(2)}, u32[]{:S(2)}) %collective-permute-start.3) | collective-permute-done | bytes 393248 | tf_op jit(solution)/shard_map/ppermute | solution.py:20
  180.6 6.4 %psum.286 = f32[384]{0:T(512)S(1)} all-reduce(f32[384]{0:T(512)S(1)} %get-tuple-element.44), channel_id=1, replica_groups=mesh['dp_0'=2,'dp_1'=4,'seq_0'=4,'seq_1'=2,'seq_2'=2] {'dp_0'}, use_global_device_ids=true, to_apply=%region_25.0 | all-reduce | flops 384 | bytes 3072 | tf_op jit(solution)/shard_map/psum | solution.py:25
  187.0 9.7 %psum.287 = f32[384]{0:T(512)S(1)} all-reduce(f32[384]{0:T(512)S(1)} %psum.286), channel_id=1, replica_groups=mesh['dp_0'=2,'dp_1'=4,'seq_0'=4,'seq_1'=2,'seq_2'=2] {'dp_1'}, use_global_device_ids=true, to_apply=%region_26.0 | all-reduce | flops 384 | bytes 3072 | tf_op jit(solution)/shard_map/psum | solution.py:25
  196.7 12.3 %psum.288 = f32[384]{0:T(512)S(1)} all-reduce(f32[384]{0:T(512)S(1)} %psum.287), channel_id=1, replica_groups=mesh['dp_0'=2,'dp_1'=4,'seq_0'=4,'seq_1'=2,'seq_2'=2] {'seq_0'}, use_global_device_ids=true, to_apply=%region_27.0 | all-reduce | flops 384 | bytes 3072 | tf_op jit(solution)/shard_map/psum | solution.py:25
  223.0 7.7 %psum.292 = f32[384]{0:T(512)S(1)} all-reduce(f32[384]{0:T(512)S(1)} %psum.291), channel_id=1, replica_groups=mesh['dp_0'=2,'dp_1'=4,'seq_0'=4,'seq_1'=2,'seq_2'=2] {'dp_1'}, use_global_device_ids=true, to_apply=%region_32.0 | all-reduce | flops 384 | bytes 3072 | tf_op jit(solution)/shard_map/psum | solution.py:25
  230.7 7.7 %psum.293 = f32[384]{0:T(512)S(1)} all-reduce(f32[384]{0:T(512)S(1)} %psum.292), channel_id=1, replica_groups=mesh['dp_0'=2,'dp_1'=4,'seq_0'=4,'seq_1'=2,'seq_2'=2] {'seq_0'}, use_global_device_ids=true, to_apply=%region_33.0 | all-reduce | flops 384 | bytes 3072 | tf_op jit(solution)/shard_map/psum | solution.py:25
  246.6 13.0 %convert_reduce_fusion = (f32[5313]{0:T(1024)}, bf16[512,5313]{0,1:T(8,128)(2,1)S(1)}) fusion(s32[1,512,5313]{1,0,2:T(1,128)} %param.13, f32[5313]{0:T(1024)S(1)} %copy-done.42, bf16[384,5313]{0,1:T(8,128)(2,1)} %param.11, f32[1,512,384]{2,1,0:T(8,128)S(1)} %get-tuple-element.45, f32[384]{0:T(512)S(1)} %get-tuple-element.15, f32[384]{0:T(512)S(1)} %get-tuple-element.53, ...), kind=kOutput, calls=%fused_computation.4 | convolution fusion | flops 2121758976 | bytes 21237000 | tf_op jit(solution)/shard_map/dot_general | solution.py:125
  265.7 66.6 %all-reduce.1 = (f32[384]{0:T(512)S(1)}, f32[384]{0:T(512)}) all-reduce(f32[384]{0:T(512)} %get-tuple-element.11, f32[384]{0:T(512)} %get-tuple-element.10), channel_id=1, replica_groups=mesh['dp_0'=2,'dp_1'=4,'seq_0'=4,'seq_1'=2,'seq_2'=2] {'dp_0','dp_1','se..., use_global_device_ids=true, to_apply=%region_39.0 | all-reduce | flops 768 | bytes 6144 | tf_op jit(solution)/shard_map/psum | solution.py:141
  354.1 62.5 %psum.298 = f32[768]{0:T(1024)S(1)} all-reduce(f32[768]{0:T(1024)S(1)} %pad_maximum_fusion.3), channel_id=1, replica_groups=mesh['dp_0'=2,'dp_1'=4,'seq_0'=4,'seq_1'=2,'seq_2'=2] {'dp_0','dp_1','se..., use_global_device_ids=true, to_apply=%region_42.0 | all-reduce | flops 768 | bytes 6144 | tf_op jit(solution)/shard_map/psum | solution.py:33
  423.1 8.6 %convolution_convert_fusion = bf16[384,5313]{1,0:T(8,128)(2,1)} fusion(bf16[512,5313]{0,1:T(8,128)(2,1)} %copy-done.43, f32[1,512,384]{2,1,0:T(8,128)S(1)} %get-tuple-element.45, f32[384]{0:T(512)S(1)} %copy-done.40, f32[384]{0:T(512)S(1)} %copy-done.36, f32[384]{0:T(512)S(1)} %copy-done.19, f32[384]{0:T(512)S(1)} %broadcast_multiply_fusion.3), kind=kOutput, calls=%fused_computation.5 | convolution fusion | flops 2104762752 | bytes 10313472 | tf_op jit(solution)/shard_map/dot_general | solution.py:128
  436.6 7.2 %collective-permute-done.7 = bf16[1,512,384]{2,1,0:T(8,128)(2,1)S(1)} collective-permute-done((bf16[1,512,384]{2,1,0:T(8,128)(2,1)S(1)}, bf16[1,512,384]{2,1,0:T(8,128)(2,1)S(1)}, u32[]{:S(2)}, u32[]{:S(2)}) %collective-permute-start.7) | collective-permute-done | bytes 393248 | tf_op jit(solution)/shard_map/ppermute | solution.py:20
  452.9 64.0 %all-reduce = (f32[768]{0:T(1024)S(1)}, f32[5313]{0:T(1024)}) all-reduce(f32[768]{0:T(1024)S(1)} %pad_maximum_fusion.4, f32[5313]{0:T(1024)S(1)} %copy-done.16), channel_id=1, replica_groups=mesh['dp_0'=2,'dp_1'=4,'seq_0'=4,'seq_1'=2,'seq_2'=2] {'dp_0','dp_1','se..., use_global_device_ids=true, to_apply=%region_45.0 | all-reduce | flops 6081 | bytes 48648 | tf_op jit(solution)/shard_map/psum | solution.py:33
  519.3 61.9 %all-reduce.6.cloned.1.call-done = (f32[1,3,384,384]{3,2,1,0:T(8,128)}, f32[1,3,384,384]{3,2,1,0:T(8,128)}) async-done(((f32[1,3,384,384]{3,2,1,0:T(8,128)}, f32[1,3,384,384]{3,2,1,0:T(8,128)}), (f32[1,3,384,384]{3,2,1,0:T(8,128)}, f32[1,3,384,384]{3,2,1,0:T(8,128)})) %all-reduce.6.cloned.1.call-update) | async-done | bytes 3538960 | tf_op jit(solution)/shard_map/psum | solution.py:184
  585.2 46.3 %all-reduce.7 = f32[24,5313]{1,0:T(8,128)} all-reduce(bf16[24,5313]{1,0:T(8,128)(2,1)} %reduce-scatter.2.cloned.1.call-done), channel_id=1, replica_groups=mesh['dp_0'=2,'dp_1'=4,'seq_0'=4,'seq_1'=2,'seq_2'=2] {'dp_0','dp_1'}, use_global_device_ids=true, to_apply=%region_49.0 | all-reduce | flops 127512 | bytes 765072 | tf_op jit(solution)/shard_map/psum | solution.py:135
  (173 shorter events, 154.9 us)
Async XLA Ops:
  8.0 78.3 %copy-start.1 = (bf16[2,3,384,384]{3,2,1,0:T(8,128)(2,1)S(1)}, bf16[2,3,384,384]{3,2,1,0:T(8,128)(2,1)}, u32[]{:S(2)}) copy-start(bf16[2,3,384,384]{3,2,1,0:T(8,128)(2,1)} %param.8) | copy-start | bytes 5308420
  8.0 573.1 %all-reduce.6.cloned.1.call-start = ((), (), s32[]{:S(2)}) async-start(), calls=%async_computation.2 | async-start | bytes 7077888 | tf_op jit(solution)/shard_map/psum | solution.py:184
  76.0 18.2 %copy-start.31 = (f32[384]{0:T(512)}, f32[384]{0:T(512)S(1)}, u32[]{:S(2)}) copy-start(f32[384]{0:T(512)S(1)} %get-tuple-element.16) | copy-start | bytes 4612
  76.0 84.5 %copy-start.28 = (f32[384]{0:T(512)}, f32[384]{0:T(512)S(1)}, u32[]{:S(2)}) copy-start(f32[384]{0:T(512)S(1)} %get-tuple-element.52) | copy-start | bytes 4612
  76.0 84.5 %copy-start.37 = (f32[384]{0:T(512)}, f32[384]{0:T(512)S(1)}, u32[]{:S(2)}) copy-start(f32[384]{0:T(512)S(1)} %get-tuple-element.17) | copy-start | bytes 4612
  76.0 170.6 %copy-start.39 = (f32[384]{0:T(512)}, f32[384]{0:T(512)S(1)}, u32[]{:S(2)}) copy-start(f32[384]{0:T(512)S(1)} %get-tuple-element.15) | copy-start | bytes 4612
  76.0 183.6 %copy-start.35 = (f32[384]{0:T(512)}, f32[384]{0:T(512)S(1)}, u32[]{:S(2)}) copy-start(f32[384]{0:T(512)S(1)} %get-tuple-element.53) | copy-start | bytes 4612
  80.3 13.5 %collective-permute-start.1 = (bf16[1,512,384]{2,1,0:T(8,128)(2,1)S(1)}, bf16[1,512,384]{2,1,0:T(8,128)(2,1)S(1)}, u32[]{:S(2)}, u32[]{:S(2)}) collective-permute-start(bf16[1,512,384]{2,1,0:T(8,128)(2,1)S(1)} %get-tuple-element.28), channel_id=1, source_target_pairs={{4,0},{5,1},{6,2},{7,3},{8,4},{9,5},{10,6},{11,7},{12,8},{13,9},{1... | collective-permute-start | bytes 1179656 | tf_op jit(solution)/shard_map/ppermute | solution.py:20
  81.7 13.2 %collective-permute-start = (bf16[1,512,384]{2,1,0:T(8,128)(2,1)S(1)}, bf16[1,512,384]{2,1,0:T(8,128)(2,1)S(1)}, u32[]{:S(2)}, u32[]{:S(2)}) collective-permute-start(bf16[1,512,384]{2,1,0:T(8,128)(2,1)S(1)} %get-tuple-element.28), channel_id=1, source_target_pairs={{0,4},{1,5},{2,6},{3,7},{4,8},{5,9},{6,10},{7,11},{8,12},{9,13},{1... | collective-permute-start | bytes 1179656 | tf_op jit(solution)/shard_map/ppermute | solution.py:20
  163.2 14.6 %collective-permute-start.3 = (bf16[1,512,384]{2,1,0:T(8,128)(2,1)S(1)}, bf16[1,512,384]{2,1,0:T(8,128)(2,1)S(1)}, u32[]{:S(2)}, u32[]{:S(2)}) collective-permute-start(bf16[1,512,384]{2,1,0:T(8,128)(2,1)S(1)} %get-tuple-element.26), channel_id=1, source_target_pairs={{8,0},{9,1},{10,2},{11,3},{12,4},{13,5},{14,6},{15,7},{24,16},{25,... | collective-permute-start | bytes 1179656 | tf_op jit(solution)/shard_map/ppermute | solution.py:20
  164.5 14.5 %collective-permute-start.2 = (bf16[1,512,384]{2,1,0:T(8,128)(2,1)S(1)}, bf16[1,512,384]{2,1,0:T(8,128)(2,1)S(1)}, u32[]{:S(2)}, u32[]{:S(2)}) collective-permute-start(bf16[1,512,384]{2,1,0:T(8,128)(2,1)S(1)} %get-tuple-element.26), channel_id=1, source_target_pairs={{0,8},{1,9},{2,10},{3,11},{4,12},{5,13},{6,14},{7,15},{16,24},{17,... | collective-permute-start | bytes 1179656 | tf_op jit(solution)/shard_map/ppermute | solution.py:20
  178.6 68.0 %copy-start.42 = (f32[5313]{0:T(1024)S(1)}, f32[5313]{0:T(1024)}, u32[]{:S(2)}) copy-start(f32[5313]{0:T(1024)} %param.12) | copy-start | bytes 63760
  265.7 74.4 %copy-start.4 = (bf16[1,512,384]{2,1,0:T(8,128)(2,1)S(1)}, bf16[1,512,384]{2,1,0:T(8,128)(2,1)}, u32[]{:S(2)}) copy-start(bf16[1,512,384]{2,1,0:T(8,128)(2,1)} %copy-done.3) | copy-start | bytes 1179652
  334.6 12.1 %collective-permute-start.5 = (bf16[1,512,384]{2,1,0:T(8,128)(2,1)S(1)}, bf16[1,512,384]{2,1,0:T(8,128)(2,1)S(1)}, u32[]{:S(2)}, u32[]{:S(2)}) collective-permute-start(bf16[1,512,384]{2,1,0:T(8,128)(2,1)S(1)} %fusion.102), channel_id=1, source_target_pairs={{0,8},{1,9},{2,10},{3,11},{4,12},{5,13},{6,14},{7,15},{16,24},{17,... | collective-permute-start | bytes 1179656 | tf_op jit(solution)/shard_map/ppermute | solution.py:20
  338.6 13.7 %collective-permute-start.4 = (bf16[1,512,384]{2,1,0:T(8,128)(2,1)S(1)}, bf16[1,512,384]{2,1,0:T(8,128)(2,1)S(1)}, u32[]{:S(2)}, u32[]{:S(2)}) collective-permute-start(bf16[1,512,384]{2,1,0:T(8,128)(2,1)S(1)} %fusion.102), channel_id=1, source_target_pairs={{8,0},{9,1},{10,2},{11,3},{12,4},{13,5},{14,6},{15,7},{24,16},{25,... | collective-permute-start | bytes 1179656 | tf_op jit(solution)/shard_map/ppermute | solution.py:20
  422.5 162.7 %reduce-scatter.2.cloned.1.call-start = ((), (), s32[]{:S(2)}) async-start(), calls=%async_computation.1 | async-start | bytes 4386816 | tf_op jit(solution)/shard_map/reduce_scatter | solution.py:127
  431.8 19.2 %copy-start.14 = (f32[1,512,384]{2,1,0:T(8,128)S(1)}, f32[1,512,384]{2,1,0:T(8,128)}, u32[]{:S(2)}) copy-start(f32[1,512,384]{2,1,0:T(8,128)} %get-tuple-element.29) | copy-start | bytes 2359300
  431.8 19.2 %copy-start.25 = (f32[384]{0:T(512)S(1)}, f32[384]{0:T(512)}, u32[]{:S(2)}) copy-start(f32[384]{0:T(512)} %copy-done.24) | copy-start | bytes 4612
  431.8 19.2 %copy-start.27 = (f32[384]{0:T(512)S(1)}, f32[384]{0:T(512)}, u32[]{:S(2)}) copy-start(f32[384]{0:T(512)} %copy-done.26) | copy-start | bytes 4612
  431.8 19.2 %copy-start.32 = (f32[384]{0:T(512)S(1)}, f32[384]{0:T(512)}, u32[]{:S(2)}) copy-start(f32[384]{0:T(512)} %copy-done.31) | copy-start | bytes 4612
  431.8 12.0 %collective-permute-start.7 = (bf16[1,512,384]{2,1,0:T(8,128)(2,1)S(1)}, bf16[1,512,384]{2,1,0:T(8,128)(2,1)S(1)}, u32[]{:S(2)}, u32[]{:S(2)}) collective-permute-start(bf16[1,512,384]{2,1,0:T(8,128)(2,1)S(1)} %get-tuple-element.24), channel_id=1, source_target_pairs={{0,4},{1,5},{2,6},{3,7},{4,8},{5,9},{6,10},{7,11},{8,12},{9,13},{1... | collective-permute-start | bytes 1179656 | tf_op jit(solution)/shard_map/ppermute | solution.py:20
  433.8 17.1 %collective-permute-start.6 = (bf16[1,512,384]{2,1,0:T(8,128)(2,1)S(1)}, bf16[1,512,384]{2,1,0:T(8,128)(2,1)S(1)}, u32[]{:S(2)}, u32[]{:S(2)}) collective-permute-start(bf16[1,512,384]{2,1,0:T(8,128)(2,1)S(1)} %get-tuple-element.24), channel_id=1, source_target_pairs={{4,0},{5,1},{6,2},{7,3},{8,4},{9,5},{10,6},{11,7},{12,8},{13,9},{1... | collective-permute-start | bytes 1179656 | tf_op jit(solution)/shard_map/ppermute | solution.py:20
  451.0 67.2 %copy-start.5 = (f32[1,512,384]{2,1,0:T(8,128)S(1)}, f32[1,512,384]{2,1,0:T(8,128)}, u32[]{:S(2)}) copy-start(f32[1,512,384]{2,1,0:T(8,128)} %get-tuple-element.25) | copy-start | bytes 2359300
  451.0 67.2 %copy-start.30 = (f32[384]{0:T(512)S(1)}, f32[384]{0:T(512)}, u32[]{:S(2)}) copy-start(f32[384]{0:T(512)} %get-tuple-element.36) | copy-start | bytes 4612
  (30 other events, 204.8 us)
Sparse Core Ops, SparseCore 0:
  422.6 158.5 all-reduce.5
Sparse Core Ops, SparseCore 1:
  431.9 64.7 reduce-scatter.1
where the time goes:
time: 641 us; the launch traced here: 639 us
  blocking collectives  433 us (68%)
  waiting for transfers between devices  98.4 us (15%)
  matrix products  40.8 us (6%)
  other arithmetic  24.6 us (4%)
  starting transfers between devices  22.3 us (3%)
  between operations  16.1 us (3%)
    psum x30, blocking collectives, one_axis_at_a_time(): array = lax.psum(array, axis)  194 us
    psum x2, blocking collectives, in_one(): subtotal = lax.psum(jnp.concatenate([a.ravel() for a in arrays]), axis)  127 us
    psum x1, blocking collectives, on_device(): lax.psum((local_bias_part, jnp.sum(preact_gradient, axis=(0, 1)), jnp.sum...  66.6 us
    psum x1, waiting for transfers between devices, on_device(): conv_grads[layer_number] = lax.psum(local_conv, DP_SEQ)  61.9 us
    psum x1, blocking collectives, on_device(): grad_head = lax.psum(partial_rows, DP)  46.3 us
    ppermute x8, waiting for transfers between devices, from_behind(): return lax.ppermute(block, axis, route)  36.5 us
    ppermute x8, starting transfers between devices, from_behind(): return lax.ppermute(block, axis, route)  22.2 us
    dot_general x1, matrix products, on_device(): jnp.dot(rows, head_weight, preferred_element_type=jnp.float32) + head_bias  13 us
  transfers between devices with their start and end apart: 10, of which 9 were waited for; matrix products, arithmetic and copies ran while one was open for 4% of the time, Pallas kernels for 0%

commit v1 on v0

v1 whole, which is shorter than its diff:
```python
import functools
import math

import jax
import jax.numpy as jnp
from jax import lax
from jax.experimental import pallas as pl
from jax.experimental.pallas import tpu as pltpu
from jax.sharding import PartitionSpec as P

MESH = pl.DeviceIdType.MESH
F32 = jnp.float32
BF16 = jnp.bfloat16
EPS = 1e-05
C = 384
R = 512
Q = 128
TW = 768
CH = 32
PAD = 256
NDEV = 128


def nn(a, b):
    return lax.dot_general(a, b, (((1,), (0,)), ((), ())), preferred_element_type=F32)


def nt(a, b):
    return lax.dot_general(a, b, (((1,), (1,)), ((), ())), preferred_element_type=F32)


def fold(v):
    return v.reshape(v.shape[0] // 8, 8, v.shape[1]).sum(axis=0)


def cdf_of(pre):
    return 0.5 * (1.0 + lax.erf(pre * math.sqrt(0.5)))


def slope_of(pre):
    return cdf_of(pre) + pre * (jnp.exp(-0.5 * pre * pre) * (1.0 / math.sqrt(2.0 * math.pi)))


def kernel(
    seq_ref, gain_ref, shift_ref, hb_ref, cw_hbm, hw_hbm, tg_hbm,
    gin_ref, ggain_ref, gshift_ref, ghead_ref, gbias_ref, gconv_ref,
    cw, hw, tg, xq, x1, x2, act0, act1, actT0, actT1, hs, h, hT, dz, dhacc, dhs, dhq, gp0, gp1, gp2, gpad, g, dpre, asend, arecv,
    b1, b2, load_sem, s1_sem, s2_sem, r1_sem, r2_sem, as_sem, ar_sem,
):
    dp = lax.axis_index("dp")
    sq = lax.axis_index("seq")
    x, zl, core = sq // 4, (sq // 2) % 2, sq % 2
    zh, y = dp // 4, dp % 4
    me1 = x * 2 + core
    me2 = y * 4 + zh * 2 + zl

    loads = [
        pltpu.make_async_copy(cw_hbm, cw, load_sem.at[0]),
        pltpu.make_async_copy(hw_hbm, hw, load_sem.at[1]),
        pltpu.make_async_copy(tg_hbm, tg, load_sem.at[2]),
    ]
    for cp in loads:
        cp.start()

    def peer1(d):
        slot = lax.rem(me1 + d, 8)
        return slot, (dp, (slot // 2) * 4 + zl * 2 + slot % 2)

    def peer2(d):
        slot = lax.rem(me2 + d, 16)
        return slot, (((slot // 2) % 2) * 4 + slot // 4, x * 4 + (slot % 2) * 2 + core)

    def peerx(d):
        slot = lax.rem(x + d, 4)
        return slot, (dp, slot * 4 + zl * 2 + core)

    barrier = pltpu.get_barrier_semaphore()

    @pl.loop(1, 8)
    def _(d):
        pl.semaphore_signal(barrier, inc=1, device_id=peer1(d)[1], device_id_type=MESH)

    @pl.loop(1, 16)
    def _(d):
        pl.semaphore_signal(barrier, inc=1, device_id=peer2(d)[1], device_id_type=MESH)

    def exchange(buf, k, me, count, peer, ssem, rsem, do):
        def cp(d):
            slot, dev = peer(d)
            return slot, dev

        if do == "start":
            @pl.loop(1, count)
            def _(d):
                slot, dev = peer(d)
                pltpu.make_async_remote_copy(
                    src_ref=buf.at[k, me], dst_ref=buf.at[k, me], send_sem=ssem.at[slot], recv_sem=rsem.at[k, me],
                    device_id=dev, device_id_type=MESH,
                ).start()
        else:
            @pl.loop(1, count)
            def _(d):
                slot, dev = peer(d)
                pltpu.make_async_remote_copy(
                    src_ref=buf.at[k, me], dst_ref=buf.at[k, slot], send_sem=ssem.at[slot], recv_sem=rsem.at[k, slot],
                    device_id=dev, device_id_type=MESH,
                ).wait()

    def merge(buf, k, count, each, forward):
        parts = [buf[k, i] for i in range(count)]
        total = functools.reduce(lambda a, b: a + b, parts)
        if not forward:
            return total
        mean = total[0:1] * (1.0 / count)
        dev = functools.reduce(lambda a, b: a + b, [jnp.square(p[0:1] - mean) for p in parts])
        return jnp.concatenate([mean, total[1:2] + each * dev], axis=0)

    def sync(k, value, forward, work1=None, work2=None):
        b1[k, me1] = value
        exchange(b1, k, me1, 8, peer1, s1_sem, r1_sem, "start")
        if work1 is not None:
            work1()
        exchange(b1, k, me1, 8, peer1, s1_sem, r1_sem, "wait")
        b2[k, me2] = merge(b1, k, 8, float(R), forward)
        exchange(b2, k, me2, 16, peer2, s2_sem, r2_sem, "start")
        if work2 is not None:
            work2()
        exchange(b2, k, me2, 16, peer2, s2_sem, r2_sem, "wait")
        return merge(b2, k, 16, float(R * 8), forward)

    def a2a(n, src, dst, do):
        for d in range(1, 4):
            slot, dev = peerx(d)
            mine = pltpu.make_async_remote_copy(
                src_ref=src.at[slot], dst_ref=dst.at[x], send_sem=as_sem.at[n, d], recv_sem=ar_sem.at[n, x],
                device_id=dev, device_id_type=MESH,
            )
            if do == "start":
                mine.start()
            else:
                mine.wait_send()
                pltpu.make_async_remote_copy(
                    src_ref=src.at[slot], dst_ref=dst.at[slot], send_sem=as_sem.at[n, d], recv_sem=ar_sem.at[n, slot],
                    device_id=dev, device_id_type=MESH,
                ).wait_recv()

    def chunks(body, init=None, step=CH):
        def f(i, carry):
            return body(pl.multiple_of(i * step, step), carry)
        return lax.fori_loop(0, R // step, f, init)

    def stats(load):
        zero = jnp.zeros((8, C), F32)
        total = chunks(lambda o, acc: acc + fold(load(o)), zero)
        mean = jnp.sum(total, axis=0, keepdims=True) * (1.0 / R)
        m2 = chunks(lambda o, acc: acc + fold(jnp.square(load(o) - mean)), zero)
        return jnp.concatenate([mean, jnp.sum(m2, axis=0, keepdims=True)], axis=0)

    first = stats(lambda o: seq_ref[pl.ds(o, CH), :].astype(F32))
    pl.semaphore_wait(barrier, 22)

    for d in range(1, 4):
        slot, dev = peerx(d)
        pltpu.make_async_remote_copy(
            src_ref=seq_ref.at[pl.ds(pl.multiple_of(slot * Q, Q), Q)], dst_ref=xq.at[x], send_sem=as_sem.at[0, d],
            recv_sem=ar_sem.at[0, x], device_id=dev, device_id_type=MESH,
        ).start()

    def begin():
        xq[x] = seq_ref[pl.ds(pl.multiple_of(x * Q, Q), Q), :]
        zeros = jnp.zeros((PAD, C), BF16)
        for buf in (act0, act1, gpad):
            buf[0:PAD] = zeros
            buf[PAD + R:] = zeros
        a2a(0, xq, xq, "wait")
        loads[0].wait()

    def load0(o):
        return xq[o // Q, pl.ds(lax.rem(o, Q), CH), :].astype(F32)

    def loader(ref):
        return lambda o: ref[pl.ds(o, CH), :]

    load_x = [load0, loader(x1), loader(x2)]
    acts, actTs, gps = [act0, act1, None], [actT0, actT1], [gp0, gp1, gp2]
    norms = []

    def norm(k, moments):
        inv = lax.rsqrt(moments[1:2] * (1.0 / (R * NDEV)) + EPS)
        norms.append((moments[0:1], inv, gain_ref[k:k + 1, :], shift_ref[k:k + 1, :]))

    def xhat_at(k, o):
        mean, inv, _, _ = norms[k]
        return (load_x[k](o) - mean) * inv

    def pre_at(k, o):
        return xhat_at(k, o) * norms[k][2] + norms[k][3]

    def activate(k, store):
        def body(o, _):
            pre = pre_at(k, o)
            store(o, (pre * cdf_of(pre)).astype(BF16))
        chunks(body)

    def slopes(k):
        def body(o, _):
            gps[k][pl.ds(o, CH), :] = slope_of(pre_at(k, o))
        chunks(body)

    moments = sync(0, first, True, begin)
    norm(0, moments)
    outs = [x1, x2]
    spans = (Q, 2 * Q)
    for l in range(2):
        act, dst, span = acts[l], outs[l], spans[l]

        def keep(o, v, act=act):
            act[pl.ds(PAD + o, CH), :] = v

        activate(l, keep)
        for r in range(0, R, 256):
            acc = nn(act[pl.ds(PAD - span + r, 256), :], cw[l, 0])
            acc += nn(act[pl.ds(PAD + r, 256), :], cw[l, 1])
            acc += nn(act[pl.ds(PAD + span + r, 256), :], cw[l, 2])
            if l == 0:
                old = jnp.concatenate([xq[r // Q], xq[r // Q + 1]], axis=0).astype(F32)
            else:
                old = x1[pl.ds(r, 256), :]
            dst[pl.ds(r, 256), :] = old + acc

        def side(l=l, act=act):
            slopes(l)
            actTs[l][...] = act[pl.ds(PAD, R), :].T

        moments = sync(l + 1, stats(load_x[l + 1]), True, side)
        norm(l + 1, moments)

    def keep_h(o, v):
        hs[o // Q, pl.ds(lax.rem(o, Q), CH), :] = v

    activate(2, keep_h)
    a2a(1, hs, h, "start")
    h[x] = hs[x]
    slopes(2)
    loads[1].wait()
    loads[2].wait()
    a2a(1, hs, h, "wait")
    for k in range(4):
        hT[:, k * Q:(k + 1) * Q] = h[k].T
    scale = 1.0 / math.sqrt(R * NDEV)
    tracks = hw.shape[1]

    def tile(start, width, store_dh):
        cols = pl.ds(start, width)
        w = hw[:, cols]
        bias = hb_ref[:, cols]
        total = jnp.zeros((8, width), F32)
        for k in range(4):
            logits = nn(h[k], w) + bias
            counts = tg[pl.ds(k * Q, Q), cols].astype(F32)
            v = ((jnp.exp(logits) - counts) * scale).astype(BF16)
            dz[k * Q:(k + 1) * Q, 0:width] = v
            total = total + fold(v.astype(F32))
            store_dh(k, nt(v, w))
        gbias_ref[:, cols] = jnp.sum(total, axis=0, keepdims=True)
        ghead_ref[:, cols] = nn(hT[...], dz[:, 0:width]).astype(BF16)

    full = tracks // TW

    def put(k, v):
        dhacc[k] = v

    def add(k, v):
        dhacc[k] += v

    tile(full * TW, tracks - full * TW, put)

    @pl.loop(0, full)
    def _(t):
        tile(pl.multiple_of(t * TW, TW), TW, add)

    for k in range(4):
        dhs[k] = dhacc[k].astype(BF16)
    a2a(2, dhs, dhq, "start")
    dhq[x] = dhs[x]
    a2a(2, dhs, dhq, "wait")

    n = float(R * NDEV)

    def sums(k, load):
        def body(o, acc):
            v = load(o) * gps[k][pl.ds(o, CH), :]
            dpre[pl.ds(o, CH), :] = v
            return acc[0] + fold(v), acc[1] + fold(v * xhat_at(k, o))
        zero = jnp.zeros((8, C), F32)
        a, b = chunks(body, (zero, zero))
        return jnp.concatenate([jnp.sum(a, axis=0, keepdims=True), jnp.sum(b, axis=0, keepdims=True)], axis=0)

    def report(k, s):
        gshift_ref[k:k + 1, :] = s[0:1]
        ggain_ref[k:k + 1, :] = s[1:2]

    def dv_at(k, o, s):
        _, inv, gain, _ = norms[k]
        return gain * inv * (dpre[pl.ds(o, CH), :] - s[0:1] * (1.0 / n) - xhat_at(k, o) * (s[1:2] * (1.0 / n)))

    s = sync(3, sums(2, lambda o: dhq[o // Q, pl.ds(lax.rem(o, Q), CH), :].astype(F32)), False)
    report(2, s)

    for l in (1, 0):
        span = spans[l]

        def spread(o, _, l=l, s=s):
            v = dv_at(l + 1, o, s)
            if l == 0:
                v = v + g[pl.ds(o, CH), :]
            g[pl.ds(o, CH), :] = v
            gpad[pl.ds(PAD + o, CH), :] = v.astype(BF16)

        chunks(spread)
        for r in range(0, R, 256):
            acc = nt(gpad[pl.ds(PAD + span + r, 256), :], cw[l, 0])
            acc += nt(gpad[pl.ds(PAD + r, 256), :], cw[l, 1])
            acc += nt(gpad[pl.ds(PAD - span + r, 256), :], cw[l, 2])
            dpre[pl.ds(r, 256), :] = acc

        value = sums(l, lambda o: dpre[pl.ds(o, CH), :])

        def weights(l=l, span=span):
            for j, shift in enumerate((span, 0, -span)):
                gconv_ref[l, j] = nn(actTs[l][...], gpad[pl.ds(PAD + shift, R), :])

        def early(l=l, weights=weights):
            if l == 0:
                _, inv, gain, _ = norms[0]

                def body(o, _):
                    asend[o // Q, pl.ds(lax.rem(o, Q), CH), :] = g[pl.ds(o, CH), :] + gain * inv * dpre[pl.ds(o, CH), :]
                chunks(body)
                a2a(3, asend, arecv, "start")
                arecv[x] = asend[x]
            weights()

        s = sync(5 - l, value, False, early)
        report(l, s)

    a2a(3, asend, arecv, "wait")
    mean, inv, gain, _ = norms[0]

    def finish(o, _):
        xh = (seq_ref[pl.ds(o, CH), :].astype(F32) - mean) * inv
        part = arecv[o // Q, pl.ds(lax.rem(o, Q), CH), :]
        gin_ref[pl.ds(o, CH), :] = part - gain * inv * (s[0:1] * (1.0 / n) + xh * (s[1:2] * (1.0 / n)))
    chunks(finish)


def on_device(sequence, conv_weight, gains, shifts, head_weight, head_bias, targets):
    tracks = head_weight.shape[1]
    vmem = pl.BlockSpec(memory_space=pltpu.VMEM)
    hbm = pl.BlockSpec(memory_space=pl.ANY)
    sds = jax.ShapeDtypeStruct
    V = pltpu.VMEM
    D = pltpu.SemaphoreType.DMA
    gin, ggain, gshift, ghead, gbias, gconv = pl.pallas_call(
        kernel,
        out_shape=(
            sds((R, C), F32), sds((3, C), F32), sds((3, C), F32), sds((C, tracks), BF16), sds((1, tracks), F32),
            sds((2, 3, C, C), F32),
        ),
        in_specs=[vmem, vmem, vmem, vmem, hbm, hbm, hbm],
        out_specs=(vmem,) * 6,
        scratch_shapes=[
            V((2, 3, C, C), BF16), V((C, tracks), BF16), V((R, tracks), jnp.int32),
            V((4, Q, C), BF16), V((R, C), F32), V((R, C), F32),
            V((R + 2 * PAD, C), BF16), V((R + 2 * PAD, C), BF16), V((C, R), BF16), V((C, R), BF16),
            V((4, Q, C), BF16), V((4, Q, C), BF16), V((C, R), BF16), V((R, TW), BF16), V((4, Q, C), F32),
            V((4, Q, C), BF16), V((4, Q, C), BF16),
            V((R, C), F32), V((R, C), F32), V((R, C), F32), V((R + 2 * PAD, C), BF16), V((R, C), F32), V((R, C), F32),
            V((4, Q, C), F32), V((4, Q, C), F32),
            V((6, 8, 2, C), F32), V((6, 16, 2, C), F32),
            D((3,)), D((8,)), D((16,)), D((6, 8)), D((6, 16)), D((4, 4)), D((4, 4)),
        ],
        compiler_params=pltpu.CompilerParams(
            collective_id=0, has_side_effects=True, vmem_limit_bytes=62 * 1024 * 1024
        ),
        name="whole",
    )(sequence.reshape(R, C), gains, shifts, head_bias.reshape(1, tracks), conv_weight, head_weight,
      targets.reshape(R, tracks))
    rows = lax.psum_scatter(ghead, "seq", scatter_dimension=0, tiled=True).astype(F32)
    grad_head = lax.psum(rows, "dp")
    grad_conv, bias = lax.psum((gconv, gbias), ("dp", "seq"))
    return gin.reshape(1, R, C), grad_conv, ggain, gshift, grad_head, bias.reshape(tracks)


def solution(mesh):
    rep = P()
    return jax.shard_map(
        on_device,
        mesh=mesh,
        in_specs=(P("dp", "seq", None), rep, rep, rep, rep, rep, P("dp", "seq", None)),
        out_specs=(P("dp", "seq", None), rep, rep, rep, P("seq", None), rep),
        check_vma=False,
    )
```

time: 641 us -> 363 us (0.57)
  blocking collectives: 433 us -> 113 us
  Pallas kernels: 0 us -> 103 us
  matrix products: 40.8 us -> 0 us
  local copies, waits for them, and re-layouts: 3.4 us -> 38.3 us
  other arithmetic: 24.6 us -> 0.05 us
  starting transfers between devices: 22.3 us -> 0.08 us
    psum x34 -> x2, blocking collectives: 433 us -> 113 us  [the longest x1 66.6 us: on_device(): grad_conv, bias = lax.psum((gconv, gbias), ('dp', 'seq'))]
    pallas_call x0 -> x1, Pallas kernels: none -> 103 us  [on_device(): pl.pallas_call(kernel, out_shape=(sds((R, C), F32), sds((3, C), F32), sds...]
    dot_general x21 -> x0, matrix products: 40.8 us -> none  [the longest x1 13 us: on_device(): jnp.dot(rows, head_weight, preferred_element_type=jnp.float32) + head_bias]
    ppermute x8 -> x0, waiting for transfers between devices: 36.5 us -> none  [from_behind(): return lax.ppermute(block, axis, route)]
    unnamed x88 -> x14, local copies, waits for them, and re-layouts: 2.49 us -> 36.9 us
    psum x1, waiting for transfers between devices: 61.9 us -> 92.1 us  [on_device(): grad_conv, bias = lax.psum((gconv, gbias), ('dp', 'seq'))]
    ppermute x8 -> x0, starting transfers between devices: 22.2 us -> none  [from_behind(): return lax.ppermute(block, axis, route)]
    convert_element_type x4 -> x0, other arithmetic: 9.8 us -> none  [the longest x2 6.42 us: batch_norm_forward(): exact_gelu_fn(preactivation).astype(jnp.bfloat16)]
  transfers between devices with their start and end apart: 10 -> 2, of which waited for: 9 -> 1; matrix products, arithmetic and copies ran while one was open for 4% -> 0% of each run, Pallas kernels for 0% -> 0%
where the time goes in v1:
time: 363 us; the launch traced here: 362 us
  blocking collectives  113 us (31%)
  Pallas kernels  103 us (28%)
  waiting for transfers between devices  92.6 us (26%)
  local copies, waits for them, and re-layouts  38.3 us (11%)
  between operations  15.5 us (4%)
    pallas_call x1, Pallas kernels, on_device(): pl.pallas_call(kernel, out_shape=(sds((R, C), F32), sds((3, C), F32), sds...  103 us
    psum x1, waiting for transfers between devices, on_device(): grad_conv, bias = lax.psum((gconv, gbias), ('dp', 'seq'))  92.1 us
    psum x1, blocking collectives, on_device(): grad_conv, bias = lax.psum((gconv, gbias), ('dp', 'seq'))  66.6 us
    psum x1, blocking collectives, on_device(): grad_head = lax.psum(rows, 'dp')  46.4 us
    unnamed x14, local copies, waits for them, and re-layouts  36.9 us
  transfers between devices with their start and end apart: 2, of which 1 were waited for; matrix products, arithmetic and copies ran while one was open for 0% of the time, Pallas kernels for 0%

profile of v1, /device:TPU:0, one launch (start us, length us, event | category | flops | bytes accessed | tf_op | source)
XLA Modules:
  0.0 362.3 jit_solution(2003355879306762747)
XLA Ops:
  8.0 0.0 all-reduce.3.cloned.1.call-start
  8.0 1.4 reshape.28.hb_ref
  9.4 6.4 %copy.14.hw_hbm = bf16[384,5313]{1,0:T(8,128)(2,1)} copy(bf16[384,5313]{0,1:T(8,128)(2,1)} %param.11) | data formatting | bytes 8160768 | tf_op args[4]
  15.8 24.3 %copy.13 = s32[1,512,5313]{2,1,0:T(8,128)} copy(s32[1,512,5313]{1,0,2:T(1,128)} %param.13) | data formatting | bytes 21762048 | tf_op args[6]
  40.1 102.8 %whole.1 = (f32[512,384]{1,0:T(8,128)}, f32[3,384]{1,0:T(4,128)}, f32[3,384]{1,0:T(4,128)}, bf16[384,5313]{1,0:T(8,128)(2,1)}, f32[1,5313]{1,0:T(1,128)}, /*index=5*/f32[2,3,384,384]{3,2,1,0:T(8,128)}) custom-call(bf16[512,384]{1,0:T(8,128)(2,1)} %bitcast.5, f32[3,384]{1,0:T(4,128)} %gain_ref.1, f32[3,384]{1,0:T(4,128)} %shift_ref.1, ...), custom_call_target="tpu_custom_call" | custom-call | tf_op jit(solution)/shard_map/whole/pallas_call | solution.py:364
  142.9 0.0 copy-start.1
  142.9 0.0 copy-start
  142.9 0.0 all-reduce.3.cloned.1.call-update
  143.0 0.0 reduce-scatter.2.cloned.1.call-start
  143.0 0.5 reduce-scatter.2.cloned.1.call-update
  143.5 0.1 copy-done.1
  143.6 0.1 reduce
  143.7 66.6 %psum.23 = f32[5313]{0:T(1024)} all-reduce(f32[5313]{0:T(1024)S(1)} %reduce), channel_id=1, replica_groups=mesh['dp'=8,'seq'=16] {'dp','seq'}, use_global_device_ids=true, to_apply=%region_3.0 | all-reduce | flops 5313 | bytes 42504 | tf_op jit(solution)/shard_map/psum | solution.py:391
  210.3 92.1 %all-reduce.3.cloned.1.call-done = f32[2,3,384,384]{3,2,1,0:T(8,128)} async-done(((f32[2,3,384,384]{3,2,1,0:T(8,128)}), f32[2,3,384,384]{3,2,1,0:T(8,128)}) %all-reduce.3.cloned.1.call-update) | async-done | bytes 3538960 | tf_op jit(solution)/shard_map/psum | solution.py:391
  302.3 0.0 reduce-scatter.2.cloned.1.call-done
  302.4 46.4 %all-reduce.4 = f32[24,5313]{1,0:T(8,128)} all-reduce(bf16[24,5313]{1,0:T(8,128)(2,1)} %reduce-scatter.2.cloned.1.call-done), channel_id=1, replica_groups=mesh['dp'=8,'seq'=16] {'dp'}, use_global_device_ids=true, to_apply=%region_2.0 | all-reduce | flops 127512 | bytes 765072 | tf_op jit(solution)/shard_map/psum | solution.py:390
  348.7 0.0 copy-done
  348.7 0.0 copy-start.3
  348.7 0.9 copy.22
  349.6 4.0 %copy.23 = f32[2,3,384,384]{3,2,1,0:T(8,128)} copy(f32[2,3,384,384]{3,2,1,0:T(8,128)} %all-reduce.3.cloned.1.call-done) | data formatting | bytes 7077888
  353.6 0.0 copy-done.3
  353.6 0.6 copy.24
  354.2 0.0 copy-done.2
  354.2 0.6 copy.25
  (1 shorter events, 0.0 us)
Async XLA Ops:
  8.0 294.3 %all-reduce.3.cloned.1.call-start = ((), (), s32[]{:S(2)}) async-start(), calls=%async_computation.1 | async-start | bytes 7077888 | tf_op jit(solution)/shard_map/psum | solution.py:391
  142.9 0.7 copy-start.1
  142.9 205.8 %copy-start = (f32[512,384]{1,0:T(8,128)S(1)}, f32[512,384]{1,0:T(8,128)}, u32[]{:S(2)}) copy-start(f32[512,384]{1,0:T(8,128)} %get-tuple-element.12) | copy-start | bytes 2359300
  143.0 159.4 %reduce-scatter.2.cloned.1.call-start = ((), (), s32[]{:S(2)}) async-start(), calls=%async_computation.2 | async-start | bytes 4386816 | tf_op jit(solution)/shard_map/reduce_scatter | solution.py:389
  348.7 4.9 %copy-start.3 = (f32[3,384]{1,0:T(4,128)S(1)}, f32[3,384]{1,0:T(4,128)}, u32[]{:S(2)}) copy-start(f32[3,384]{1,0:T(4,128)} %get-tuple-element.26) | copy-start | bytes 13828
  348.7 5.5 %copy-start.2 = (f32[3,384]{1,0:T(4,128)S(1)}, f32[3,384]{1,0:T(4,128)}, u32[]{:S(2)}) copy-start(f32[3,384]{1,0:T(4,128)} %get-tuple-element.27) | copy-start | bytes 13828
Sparse Core Ops, SparseCore 0:
  143.1 159.2 all-reduce.2
Sparse Core Ops, SparseCore 1:
  145.8 66.6 reduce-scatter.1

commit v2 on v1

--- a/solution.py
+++ b/solution.py
@@ -44,8 +44,13 @@
 def kernel(
     seq_ref, gain_ref, shift_ref, hb_ref, cw_hbm, hw_hbm, tg_hbm,
     gin_ref, ggain_ref, gshift_ref, ghead_ref, gbias_ref, gconv_ref,
-    cw, hw, tg, xq, x1, x2, act0, act1, actT0, actT1, hs, h, hT, dz, dhacc, dhs, dhq, gp0, gp1, gp2, gpad, g, dpre, asend, arecv,
-    b1, b2, load_sem, s1_sem, s2_sem, r1_sem, r2_sem, as_sem, ar_sem,
+    cw, wt, wtail, w, tg, ttail, bcol, hbp, xq, x1, x2, act0, act1, actT0, actT1, hs, h, hT, hP, hPb, dz, dhacc, dhs, dhq,
+    gp0, gp1, gp2, gpad, g, dpre, asend, arecv, b1, b2, bb1, bb2,
+    gsend, grecv, gown, xsend, xrecv, zown, zsend, zrecv, dsend, drecv, fall,
+    cfull, csend, crecv, cx, cxr, cy, cyr, cz, ca, cb,
+    load_sem, s1_sem, s2_sem, r1_sem, r2_sem, as_sem, ar_sem,
+    e1_sem, e2_sem, q1_sem, q2_sem, gcs, gcr, gxs, gxr, gzs, gzr, gds, gdr, gfs, gfr,
+    ccs, ccr, cxs, cxrs, cys, cyrs, czs, czrs, cas, cars, cbs, cbrs,
 ):
     dp = lax.axis_index("dp")
     sq = lax.axis_index("seq")
@@ -56,8 +61,10 @@
 
     loads = [
         pltpu.make_async_copy(cw_hbm, cw, load_sem.at[0]),
-        pltpu.make_async_copy(hw_hbm, hw, load_sem.at[1]),
-        pltpu.make_async_copy(tg_hbm, tg, load_sem.at[2]),
+        pltpu.make_async_copy(hw_hbm, wt, load_sem.at[1]),
+    ] + [
+        pltpu.make_async_copy(tg_hbm.at[:, 0, j * Q:(j + 1) * Q], tg.at[:, j * Q:(j + 1) * Q], load_sem.at[2 + j])
+        for j in range(4)
     ]
     for cp in loads:
         cp.start()
@@ -175,6 +182,39 @@
         a2a(0, xq, xq, "wait")
         loads[0].wait()
 
+    def prepare_bias():
+        tracks = hb_ref.shape[0]
+        hbp[...] = jnp.zeros(hbp.shape, F32)
+        last = tracks // Q * Q
+        for i in range(tracks // Q):
+            hbp[i:i + 1, :] = hb_ref[pl.ds(i * Q, Q)].reshape(1, Q)
+        hbp[tracks // Q:tracks // Q + 1, 0:tracks - last] = hb_ref[pl.ds(last, tracks - last)].reshape(1, tracks - last)
+
+        @pl.loop(0, hbp.shape[0] - 6)
+        def _(i):
+            bcol[pl.ds(pl.multiple_of(i * Q, Q), Q), :] = jnp.broadcast_to(hbp[pl.ds(i, 1), :], (Q, Q)).T
+
+    def prepare_weights():
+        loads[1].wait()
+        tracks = wt.shape[0]
+        edge = tracks // 256 * 256
+        wtail[...] = jnp.zeros(wtail.shape, BF16)
+        wtail[0:tracks - edge] = wt[edge:tracks]
+
+        @pl.loop(0, tracks // 256)
+        def _(i):
+            o = pl.multiple_of(i * 256, 256)
+            w[:, pl.ds(o, 256)] = wt[pl.ds(o, 256), :].T
+        w[:, edge:edge + 256] = wtail[...].T
+
+    def prepare_counts():
+        for cp in loads[2:]:
+            cp.wait()
+        tracks = tg.shape[0]
+        edge = tracks // 256 * 256
+        ttail[...] = jnp.zeros(ttail.shape, jnp.int32)
+        ttail[0:tracks - edge] = tg[edge:tracks]
+
     def load0(o):
         return xq[o // Q, pl.ds(lax.rem(o, Q), CH), :].astype(F32)
 
@@ -207,7 +247,7 @@
             gps[k][pl.ds(o, CH), :] = slope_of(pre_at(k, o))
         chunks(body)
 
-    moments = sync(0, first, True, begin)
+    moments = sync(0, first, True, begin, prepare_bias)
     norm(0, moments)
     outs = [x1, x2]
     spans = (Q, 2 * Q)
@@ -232,8 +272,20 @@
             slopes(l)
             actTs[l][...] = act[pl.ds(PAD, R), :].T
 
-        moments = sync(l + 1, stats(load_x[l + 1]), True, side)
+        moments = sync(l + 1, stats(load_x[l + 1]), True, side, (prepare_weights, prepare_counts)[l])
         norm(l + 1, moments)
+
+    tracks = wt.shape[0]
+    full = tracks // TW
+    rest = tracks - full * TW
+    tiles = full + 1
+    half = C // 2
+    other = (dp, sq + 1 - 2 * core)
+
+    def rcopy(src, dst, ssem, rsem, dev):
+        return pltpu.make_async_remote_copy(
+            src_ref=src, dst_ref=dst, send_sem=ssem, recv_sem=rsem, device_id=dev, device_id_type=MESH
+        )
 
     def keep_h(o, v):
         hs[o // Q, pl.ds(lax.rem(o, Q), CH), :] = v
@@ -242,48 +294,224 @@
     a2a(1, hs, h, "start")
     h[x] = hs[x]
     slopes(2)
-    loads[1].wait()
-    loads[2].wait()
     a2a(1, hs, h, "wait")
     for k in range(4):
-        hT[:, k * Q:(k + 1) * Q] = h[k].T
+        part = h[k].T
+        hT[:, k * Q:(k + 1) * Q] = part
+        wide = part.astype(F32)
+        for s in range(16):
+            sx, sz, sc = s // 4, (s // 2) % 2, s % 2
+            to = jnp.where(core == sc, half, 0) + sx * 48 + sz * 24
+            hP[pl.ds(pl.multiple_of(to, 8), 24), k * Q:(k + 1) * Q] = wide[24 * s:24 * s + 24]
+    hPb[0:C] = hP[...].astype(BF16)
+    ones_row = lax.broadcasted_iota(jnp.int32, (16, R), 0) == 0
+    hPb[C:C + 16] = jnp.where(ones_row, 1.0, 0.0).astype(BF16)
     scale = 1.0 / math.sqrt(R * NDEV)
-    tracks = hw.shape[1]
-
-    def tile(start, width, store_dh):
-        cols = pl.ds(start, width)
-        w = hw[:, cols]
-        bias = hb_ref[:, cols]
-        total = jnp.zeros((8, width), F32)
+
+    def piece(rows, counts, bias, at, live):
+        v = nn(rows, hT[...])
+        for j in range(4):
+            z = v[:, j * Q:(j + 1) * Q] + bias
+            e = (jnp.exp(z) - counts[:, j * Q:(j + 1) * Q].astype(F32)) * scale
+            if live is not None:
+                e = jnp.where(lax.broadcasted_iota(jnp.int32, e.shape, 0) < live, e, 0.0)
+            dz[at:at + 256, j * Q:(j + 1) * Q] = e.astype(BF16)
+
+    def tile(t, start, tail, first):
+        for i in range(3):
+            o = start + i * 256 if tail else pl.multiple_of(start + i * 256, 256)
+            if tail and i == 2:
+                piece(wtail[...], ttail[...], bcol[pl.ds(o, 256), :], i * 256, rest - 512)
+            else:
+                piece(wt[pl.ds(o, 256), :], tg[pl.ds(o, 256), :], bcol[pl.ds(o, 256), :], i * 256, None)
+        part = nt(hPb[...], dz[...])
+        gsend[t] = part[0:half].astype(BF16)
+        gown[1 if tail else t % 2] = part[half:C]
+        bb1[0, me1, pl.ds(t, 1), :] = part[C:C + 1]
+        add = nn(w[:, pl.ds(start if tail else pl.multiple_of(start, TW), TW)], dz[...])
+        dhacc[...] = add if first else dhacc[...] + add
+        rcopy(gsend.at[t], grecv.at[t], gcs.at[t], gcr.at[t], other).start()
+
+    def chip(t):
+        rcopy(gsend.at[t], grecv.at[t], gcs.at[t], gcr.at[t], other).wait()
+        slot = jnp.where(t == full, 1, t % 2)
         for k in range(4):
-            logits = nn(h[k], w) + bias
-            counts = tg[pl.ds(k * Q, Q), cols].astype(F32)
-            v = ((jnp.exp(logits) - counts) * scale).astype(BF16)
-            dz[k * Q:(k + 1) * Q, 0:width] = v
-            total = total + fold(v.astype(F32))
-            store_dh(k, nt(v, w))
-        gbias_ref[:, cols] = jnp.sum(total, axis=0, keepdims=True)
-        ghead_ref[:, cols] = nn(hT[...], dz[:, 0:width]).astype(BF16)
-
-    full = tracks // TW
-
-    def put(k, v):
-        dhacc[k] = v
-
-    def add(k, v):
-        dhacc[k] += v
-
-    tile(full * TW, tracks - full * TW, put)
+            xsend[t, k] = (gown[slot, k * 48:(k + 1) * 48] + grecv[t, k * 48:(k + 1) * 48].astype(F32)).astype(BF16)
+
+    def xstart(t):
+        for d in range(1, 4):
+            slot, dev = peerx(d)
+            rcopy(xsend.at[t, slot], xrecv.at[t, x], gxs.at[t, slot], gxr.at[t, x], dev).start()
+
+    zdev = (dp, x * 4 + (1 - zl) * 2 + core)
+
+    def zstart(t):
+        total = xsend[t, x].astype(F32)
+        for d in range(1, 4):
+            slot, dev = peerx(d)
+            rcopy(xsend.at[t, slot], xrecv.at[t, slot], gxs.at[t, slot], gxr.at[t, slot], dev).wait()
+            total = total + xrecv[t, slot].astype(F32)
+        low, high = total[0:24], total[24:48]
+        mine = zl == 0
+        zown[t] = jnp.where(mine, low, high)
+        zsend[t] = jnp.where(mine, high, low).astype(BF16)
+        rcopy(zsend.at[t], zrecv.at[t], gzs.at[t], gzr.at[t], zdev).start()
+
+    def dstart(t):
+        rcopy(zsend.at[t], zrecv.at[t], gzs.at[t], gzr.at[t], zdev).wait()
+        total = (zown[t] + zrecv[t].astype(F32)).astype(BF16)
+        dsend[t] = total
+
+        @pl.when(dp != t)
+        def _():
+            rcopy(dsend.at[t], drecv.at[dp], gds.at[t], gdr.at[dp], (t, sq)).start()
+
+    def finish_head():
+        @pl.loop(0, tiles)
+        def _(t):
+            @pl.when(dp != t)
+            def _():
+                rcopy(dsend.at[t], drecv.at[dp], gds.at[t], gdr.at[dp], (t, sq)).wait_send()
+
+        @pl.when(dp < tiles)
+        def _():
+            total = dsend[dp].astype(F32)
+            for d in range(1, 8):
+                slot = lax.rem(dp + d, 8)
+                rcopy(dsend.at[dp], drecv.at[slot], gds.at[dp], gdr.at[slot], (slot, sq)).wait_recv()
+                total = total + drecv[slot].astype(F32)
+            fall[dp] = total
+            for d in range(1, 8):
+                slot = lax.rem(dp + d, 8)
+                rcopy(fall.at[dp], fall.at[dp], gfs.at[slot], gfr.at[dp], (slot, sq)).start()
+
+    def collect_head():
+        @pl.when(dp < tiles)
+        def _():
+            for d in range(1, 8):
+                slot = lax.rem(dp + d, 8)
+                rcopy(fall.at[dp], fall.at[dp], gfs.at[slot], gfr.at[dp], (slot, sq)).wait_send()
+
+        for t in range(tiles):
+            @pl.when(dp != t)
+            def _():
+                rcopy(fall.at[t], fall.at[t], gfs.at[0], gfr.at[t], (t, sq)).wait_recv()
+        for t in range(full):
+            ghead_ref[:, t * TW:(t + 1) * TW] = fall[t]
+        ghead_ref[:, full * TW:tracks] = fall[full][:, 0:rest]
+
+    def bias_start():
+        exchange(bb1, 0, me1, 8, peer1, e1_sem, q1_sem, "start")
+
+    def bias_middle():
+        exchange(bb1, 0, me1, 8, peer1, e1_sem, q1_sem, "wait")
+        bb2[0, me2] = functools.reduce(lambda a, b: a + b, [bb1[0, i] for i in range(8)])
+        exchange(bb2, 0, me2, 16, peer2, e2_sem, q2_sem, "start")
+
+    def bias_end():
+        exchange(bb2, 0, me2, 16, peer2, e2_sem, q2_sem, "wait")
+        gbias_ref[...] = functools.reduce(lambda a, b: a + b, [bb2[0, i] for i in range(16)])
+
+    bb1[0, me1] = jnp.zeros((8, TW), F32)
+    tile(full, full * TW, True, True)
 
     @pl.loop(0, full)
     def _(t):
-        tile(pl.multiple_of(t * TW, TW), TW, add)
+        tile(t, t * TW, False, False)
+        before = jnp.where(t == 0, full, t - 1)
+        chip(before)
+
+        @pl.when(t < 3)
+        def _():
+            xstart(before)
 
     for k in range(4):
-        dhs[k] = dhacc[k].astype(BF16)
+        dhs[k] = dhacc[:, k * Q:(k + 1) * Q].T.astype(BF16)
     a2a(2, dhs, dhq, "start")
     dhq[x] = dhs[x]
+    chip(full - 1)
     a2a(2, dhs, dhq, "wait")
+
+    HR = 3 * C // 2
+
+    def conv_start(l, span, actT):
+        for j, shift in enumerate((span, 0, -span)):
+            cfull[j * C:(j + 1) * C] = nn(actT[...], gpad[pl.ds(PAD + shift, R), :])
+        csend[l] = cfull[pl.ds(pl.multiple_of((1 - core) * HR, 64), HR), :].astype(BF16)
+        rcopy(csend.at[l], crecv.at[l], ccs.at[l], ccr.at[l], other).start()
+
+    def conv_x(l):
+        rcopy(csend.at[l], crecv.at[l], ccs.at[l], ccr.at[l], other).wait()
+        for k in range(4):
+            mine = cfull[pl.ds(pl.multiple_of(core * HR + k * 144, 16), 144), :]
+            cx[l, k] = (mine + crecv[l, k * 144:(k + 1) * 144].astype(F32)).astype(BF16)
+        for d in range(1, 4):
+            slot, dev = peerx(d)
+            rcopy(cx.at[l, slot], cxr.at[l, x], cxs.at[l, slot], cxrs.at[l, x], dev).start()
+
+    def conv_dev(i):
+        return (((i // 2) % 2) * 4 + i // 4, x * 4 + (i % 2) * 2 + core)
+
+    def conv_rs(l):
+        total = cx[l, x].astype(F32)
+        for d in range(1, 4):
+            slot, dev = peerx(d)
+            rcopy(cx.at[l, slot], cxr.at[l, slot], cxs.at[l, slot], cxrs.at[l, slot], dev).wait()
+            total = total + cxr[l, slot].astype(F32)
+        for j in range(9):
+            cy[l, j] = total[j * 16:(j + 1) * 16].astype(BF16)
+
+            @pl.when(me2 != j)
+            def _(j=j):
+                rcopy(cy.at[l, j], cyr.at[l, me2], cys.at[l, j], cyrs.at[l, me2], conv_dev(j)).start()
+
+    def conv_ag(l):
+        for j in range(9):
+            @pl.when(me2 != j)
+            def _(j=j):
+                rcopy(cy.at[l, j], cyr.at[l, me2], cys.at[l, j], cyrs.at[l, me2], conv_dev(j)).wait_send()
+
+        @pl.when(me2 < 9)
+        def _():
+            def body(d, total):
+                slot, dev = peer2(d)
+                rcopy(cyr.at[l, slot], cyr.at[l, slot], cys.at[l, 0], cyrs.at[l, slot], dev).wait_recv()
+                return total + cyr[l, slot].astype(F32)
+            total = lax.fori_loop(1, 16, body, cy[l, me2].astype(F32))
+            cz[l, me2] = total.astype(BF16)
+
+            @pl.loop(1, 16)
+            def _(d):
+                slot, dev = peer2(d)
+                rcopy(cz.at[l, me2], cz.at[l, me2], czs.at[l, slot], czrs.at[l, me2], dev).start()
+
+    def conv_xag(l):
+        @pl.when(me2 < 9)
+        def _():
+            @pl.loop(1, 16)
+            def _(d):
+                slot, dev = peer2(d)
+                rcopy(cz.at[l, me2], cz.at[l, me2], czs.at[l, slot], czrs.at[l, me2], dev).wait_send()
+
+        for j in range(9):
+            @pl.when(me2 != j)
+            def _(j=j):
+                rcopy(cz.at[l, j], cz.at[l, j], czs.at[l, 0], czrs.at[l, j], conv_dev(j)).wait_recv()
+        for d in range(1, 4):
+            slot, dev = peerx(d)
+            rcopy(cz.at[l], ca.at[l, x], cas.at[l, slot], cars.at[l, x], dev).start()
+        ca[l, x] = cz[l]
+
+    def conv_cag(l):
+        for d in range(1, 4):
+            slot, dev = peerx(d)
+            rcopy(cz.at[l], ca.at[l, slot], cas.at[l, slot], cars.at[l, slot], dev).wait()
+        rcopy(ca.at[l], cb.at[l], cbs.at[l], cbrs.at[l], other).start()
+        gconv_ref[l, core] = ca[l]
+
+    def conv_end(l):
+        rcopy(ca.at[l], cb.at[l], cbs.at[l], cbrs.at[l], other).wait()
+        gconv_ref[l, 1 - core] = cb[l]
 
     n = float(R * NDEV)
 
@@ -304,7 +532,15 @@
         _, inv, gain, _ = norms[k]
         return gain * inv * (dpre[pl.ds(o, CH), :] - s[0:1] * (1.0 / n) - xhat_at(k, o) * (s[1:2] * (1.0 / n)))
 
-    s = sync(3, sums(2, lambda o: dhq[o // Q, pl.ds(lax.rem(o, Q), CH), :].astype(F32)), False)
+    def fill31():
+        xstart(2)
+        xstart(3)
+        bias_start()
+
+    def fill32():
+        pl.loop(0, 3)(lambda i: zstart(jnp.where(i == 0, full, i - 1)))
+
+    s = sync(3, sums(2, lambda o: dhq[o // Q, pl.ds(lax.rem(o, Q), CH), :].astype(F32)), False, fill31, fill32)
     report(2, s)
 
     for l in (1, 0):
@@ -326,11 +562,7 @@
 
         value = sums(l, lambda o: dpre[pl.ds(o, CH), :])
 
-        def weights(l=l, span=span):
-            for j, shift in enumerate((span, 0, -span)):
-                gconv_ref[l, j] = nn(actTs[l][...], gpad[pl.ds(PAD + shift, R), :])
-
-        def early(l=l, weights=weights):
+        def early(l=l, span=span):
             if l == 0:
                 _, inv, gain, _ = norms[0]
 
@@ -339,9 +571,26 @@
                 chunks(body)
                 a2a(3, asend, arecv, "start")
                 arecv[x] = asend[x]
-            weights()
-
-        s = sync(5 - l, value, False, early)
+                conv_rs(1)
+                conv_start(0, span, actTs[0])
+            else:
+                conv_start(1, span, actTs[1])
+                xstart(4)
+                xstart(5)
+
+        def late(l=l):
+            if l == 1:
+                pl.loop(2, 4)(zstart)
+                pl.loop(0, 3)(lambda i: dstart(jnp.where(i == 0, full, i - 1)))
+                bias_middle()
+                conv_x(1)
+            else:
+                conv_x(0)
+                pl.loop(4, full)(zstart)
+                pl.loop(2, 4)(dstart)
+                conv_ag(1)
+
+        s = sync(5 - l, value, False, early, late)
         report(l, s)
 
     a2a(3, asend, arecv, "wait")
@@ -352,6 +601,18 @@
         part = arecv[o // Q, pl.ds(lax.rem(o, Q), CH), :]
         gin_ref[pl.ds(o, CH), :] = part - gain * inv * (s[0:1] * (1.0 / n) + xh * (s[1:2] * (1.0 / n)))
     chunks(finish)
+    pl.loop(4, full)(dstart)
+    finish_head()
+    bias_end()
+    conv_rs(0)
+    conv_xag(1)
+    conv_ag(0)
+    conv_xag(0)
+    conv_cag(1)
+    conv_cag(0)
+    collect_head()
+    conv_end(1)
+    conv_end(0)
 
 
 def on_device(sequence, conv_weight, gains, shifts, head_weight, head_bias, targets):
@@ -361,35 +622,46 @@
     sds = jax.ShapeDtypeStruct
     V = pltpu.VMEM
     D = pltpu.SemaphoreType.DMA
+    T7 = tracks // TW + 1
+    W7 = T7 * TW
+    HR = 3 * C // 2
     gin, ggain, gshift, ghead, gbias, gconv = pl.pallas_call(
         kernel,
         out_shape=(
-            sds((R, C), F32), sds((3, C), F32), sds((3, C), F32), sds((C, tracks), BF16), sds((1, tracks), F32),
-            sds((2, 3, C, C), F32),
+            sds((R, C), F32), sds((3, C), F32), sds((3, C), F32), sds((C // 16, tracks), F32), sds((8, TW), F32),
+            sds((2, 2, 4, 9, 16, C), BF16),
         ),
         in_specs=[vmem, vmem, vmem, vmem, hbm, hbm, hbm],
         out_specs=(vmem,) * 6,
         scratch_shapes=[
-            V((2, 3, C, C), BF16), V((C, tracks), BF16), V((R, tracks), jnp.int32),
+            V((2, 3, C, C), BF16), V((tracks, C), BF16), V((256, C), BF16), V((C, W7), BF16),
+            V((tracks, R), jnp.int32), V((256, R), jnp.int32), V((W7, Q), F32), V((48, Q), F32),
             V((4, Q, C), BF16), V((R, C), F32), V((R, C), F32),
             V((R + 2 * PAD, C), BF16), V((R + 2 * PAD, C), BF16), V((C, R), BF16), V((C, R), BF16),
-            V((4, Q, C), BF16), V((4, Q, C), BF16), V((C, R), BF16), V((R, TW), BF16), V((4, Q, C), F32),
-            V((4, Q, C), BF16), V((4, Q, C), BF16),
+            V((4, Q, C), BF16), V((4, Q, C), BF16), V((C, R), BF16), V((C, R), F32), V((C + 16, R), BF16), V((TW, R), BF16),
+            V((C, R), F32), V((4, Q, C), BF16), V((4, Q, C), BF16),
             V((R, C), F32), V((R, C), F32), V((R, C), F32), V((R + 2 * PAD, C), BF16), V((R, C), F32), V((R, C), F32),
             V((4, Q, C), F32), V((4, Q, C), F32),
-            V((6, 8, 2, C), F32), V((6, 16, 2, C), F32),
-            D((3,)), D((8,)), D((16,)), D((6, 8)), D((6, 16)), D((4, 4)), D((4, 4)),
+            V((6, 8, 2, C), F32), V((6, 16, 2, C), F32), V((1, 8, 8, TW), F32), V((1, 16, 8, TW), F32),
+            V((T7, 192, TW), BF16), V((T7, 192, TW), BF16), V((2, 192, TW), F32),
+            V((T7, 4, 48, TW), BF16), V((T7, 4, 48, TW), BF16), V((T7, 24, TW), F32), V((T7, 24, TW), BF16),
+            V((T7, 24, TW), BF16), V((8, 24, TW), BF16), V((8, 24, TW), BF16), V((T7, 24, TW), F32),
+            V((3 * C, C), F32), V((2, HR, C), BF16), V((2, HR, C), BF16), V((2, 4, 144, C), BF16), V((2, 4, 144, C), BF16),
+            V((2, 9, 16, C), BF16), V((2, 16, 16, C), BF16), V((2, 9, 16, C), BF16),
+            V((2, 4, 9, 16, C), BF16), V((2, 4, 9, 16, C), BF16),
+            D((6,)), D((8,)), D((16,)), D((6, 8)), D((6, 16)), D((4, 4)), D((4, 4)),
+            D((8,)), D((16,)), D((1, 8)), D((1, 16)), D((T7,)), D((T7,)), D((T7, 4)), D((T7, 4)), D((T7,)), D((T7,)),
+            D((T7,)), D((8,)), D((8,)), D((T7,)),
+            D((2,)), D((2,)), D((2, 4)), D((2, 4)), D((2, 9)), D((2, 16)), D((2, 16)), D((2, 9)), D((2, 4)), D((2, 4)),
+            D((2,)), D((2,)),
         ],
         compiler_params=pltpu.CompilerParams(
             collective_id=0, has_side_effects=True, vmem_limit_bytes=62 * 1024 * 1024
         ),
         name="whole",
-    )(sequence.reshape(R, C), gains, shifts, head_bias.reshape(1, tracks), conv_weight, head_weight,
-      targets.reshape(R, tracks))
-    rows = lax.psum_scatter(ghead, "seq", scatter_dimension=0, tiled=True).astype(F32)
-    grad_head = lax.psum(rows, "dp")
-    grad_conv, bias = lax.psum((gconv, gbias), ("dp", "seq"))
-    return gin.reshape(1, R, C), grad_conv, ggain, gshift, grad_head, bias.reshape(tracks)
+    )(sequence.reshape(R, C), gains, shifts, head_bias, conv_weight, head_weight.T, jnp.transpose(targets, (2, 0, 1)))
+    grad_conv = gconv.reshape(2, 3, C, C).astype(F32)
+    return gin.reshape(1, R, C), grad_conv, ggain, gshift, ghead, gbias.reshape(-1)[:tracks]
 
 
 def solution(mesh):

time: 363 us -> 146 us (0.40)
  blocking collectives: 113 us -> 0 us
  waiting for transfers between devices: 92.6 us -> 0 us
  local copies, waits for them, and re-layouts: 38.3 us -> 4.31 us
  Pallas kernels: 103 us -> 135 us
  between operations: 15.5 us -> 0.68 us
    psum x2 -> x0, blocking collectives: 113 us -> none  [the longest x1 66.6 us: on_device(): grad_conv, bias = lax.psum((gconv, gbias), ('dp', 'seq'))]
    psum x1 -> x0, waiting for transfers between devices: 92.1 us -> none  [on_device(): grad_conv, bias = lax.psum((gconv, gbias), ('dp', 'seq'))]
    unnamed x14 -> x12, local copies, waits for them, and re-layouts: 36.9 us -> 2.87 us
    pallas_call x1, Pallas kernels: 103 us -> 135 us  [on_device(): pl.pallas_call(kernel, out_shape=(sds((R, C), F32), sds((3, C), F32), sds...]
  transfers between devices with their start and end apart: 2 -> 0, of which waited for: 1 -> 0; matrix products, arithmetic and copies ran while one was open for 0% -> 0% of each run, Pallas kernels for 0% -> 0%
where the time goes in v2:
time: 146 us; the launch traced here: 144 us
  Pallas kernels  135 us (92%)
  local copies, waits for them, and re-layouts  4.31 us (3%)
  other arithmetic  3.52 us (2%)
    pallas_call x1, Pallas kernels, on_device(): pl.pallas_call(kernel, out_shape=(sds((R, C), F32), sds((3, C), F32), sds...  135 us
    convert_element_type x1, other arithmetic, on_device(): grad_conv = gconv.reshape(2, 3, C, C).astype(F32)  3.52 us

profile of v2, /device:TPU:0, one launch (start us, length us, event | category | flops | bytes accessed | tf_op | source)
XLA Modules:
  0.0 144.0 jit_solution(10368190112629772140)
XLA Ops:
  0.6 135.5 %whole.1 = (f32[512,384]{1,0:T(8,128)}, f32[3,384]{1,0:T(4,128)}, f32[3,384]{1,0:T(4,128)}, f32[24,5313]{1,0:T(8,128)}, f32[8,768]{1,0:T(8,128)}, /*index=5*/bf16[2,2,4,9,16,384]{5,4,3,2,1,0:T(8,128)(2,1)}) custom-call(bf16[512,384]{1,0:T(8,128)(2,1)} %bitcast.11, f32[3,384]{1,0:T(4,128)} %gain_ref.1, f32[3,384]{1,0:T(4,128)} %shift_ref.1, f32[5313]{0:T(1024)} %hb_ref.1, ...), custom_call_target="tpu_custom_call" | custom-call | tf_op jit(solution)/shard_map/whole/pallas_call | solution.py:628
  136.1 0.0 copy-start
  136.1 0.0 copy-start.3
  136.1 0.0 copy-start.2
  136.1 0.0 copy-start.1
  136.1 1.4 %reshape.26 = f32[6144]{0:T(1024)} reshape(f32[8,768]{1,0:T(8,128)} %get-tuple-element.17) | data formatting | bytes 49152 | tf_op jit(solution)/shard_map/reshape | solution.py:664
  137.6 3.5 %convert.1 = f32[2,3,384,384]{3,2,1,0:T(8,128)} convert(bf16[2,3,384,384]{3,2,1,0:T(8,128)(2,1)} %bitcast.9) | non-fusion elementwise | flops 884736 | bytes 5308416 | tf_op jit(solution)/shard_map/convert_element_type | solution.py:663
  141.1 0.0 copy-done
  141.1 0.9 copy.17
  142.0 0.0 copy-done.3
  142.0 0.6 copy.18
  142.6 0.0 copy-done.2
  142.6 0.6 copy.19
  143.2 0.0 copy-done.1
  143.2 0.8 copy.20
Async XLA Ops:
  136.1 5.0 %copy-start = (f32[512,384]{1,0:T(8,128)S(1)}, f32[512,384]{1,0:T(8,128)}, u32[]{:S(2)}) copy-start(f32[512,384]{1,0:T(8,128)} %get-tuple-element.12) | copy-start | bytes 2359300
  136.1 5.9 %copy-start.3 = (f32[3,384]{1,0:T(4,128)S(1)}, f32[3,384]{1,0:T(4,128)}, u32[]{:S(2)}) copy-start(f32[3,384]{1,0:T(4,128)} %get-tuple-element.26) | copy-start | bytes 13828
  136.1 6.5 %copy-start.2 = (f32[3,384]{1,0:T(4,128)S(1)}, f32[3,384]{1,0:T(4,128)}, u32[]{:S(2)}) copy-start(f32[3,384]{1,0:T(4,128)} %get-tuple-element.27) | copy-start | bytes 13828
  136.1 7.0 %copy-start.1 = (f32[24,5313]{1,0:T(8,128)S(1)}, f32[24,5313]{1,0:T(8,128)}, u32[]{:S(2)}) copy-start(f32[24,5313]{1,0:T(8,128)} %get-tuple-element.28) | copy-start | bytes 1530148

commit v3 on v2

v3 whole, which is shorter than its diff:
```python
import functools
import math

import jax
import jax.numpy as jnp
from jax import lax
from jax.experimental import pallas as pl
from jax.experimental.pallas import tpu as pltpu
from jax.sharding import PartitionSpec as P

MESH = pl.DeviceIdType.MESH
F32 = jnp.float32
BF16 = jnp.bfloat16
EPS = 1e-05
C = 384
R = 512
Q = 128
TW = 768
CH = 32
PAD = 256
NDEV = 128


def nn(a, b):
    return lax.dot_general(a, b, (((1,), (0,)), ((), ())), preferred_element_type=F32)


def nt(a, b):
    return lax.dot_general(a, b, (((1,), (1,)), ((), ())), preferred_element_type=F32)


def fold(v):
    return v.reshape(v.shape[0] // 8, 8, v.shape[1]).sum(axis=0)


def cdf_of(pre):
    return 0.5 * (1.0 + lax.erf(pre * math.sqrt(0.5)))


def slope_of(pre):
    return cdf_of(pre) + pre * (jnp.exp(-0.5 * pre * pre) * (1.0 / math.sqrt(2.0 * math.pi)))


def kernel(
    seq_ref, gain_ref, shift_ref, hb_ref, cw_hbm, hw_hbm, tg_hbm,
    gin_ref, ggain_ref, gshift_ref, ghead_ref, gbias_ref, gconv_ref,
    cw, wt, wtail, w, tg, ttail, bcol, hbp, xq, x1, x2, x2o, act0, act1, actT0, actT1, hT, hPb, dz, dhacc, dps, dpq,
    gp0, gp1, gpad, g, dpre, arecv, b1, b2, bb1, bb2,
    gsend, grecv, gown, xsend, xrecv, ysend, yrecv, fall, vrecv, vsend, vx,
    cfull, csend, crecv, cx, cxr, cy, cyr, cz, ca, cb,
    load_sem, s1_sem, s2_sem, r1_sem, r2_sem, as_sem, ar_sem,
    e1_sem, e2_sem, q1_sem, q2_sem, gcs, gcr, gxs, gxr, gys, gyr, gfs, gfr, hvs, hvr, hxs, hxr,
    ccs, ccr, cxs, cxrs, cys, cyrs, czs, czrs, cas, cars, cbs, cbrs,
):
    h = asend = dps
    dp = lax.axis_index("dp")
    sq = lax.axis_index("seq")
    x, zl, core = sq // 4, (sq // 2) % 2, sq % 2
    zh, y = dp // 4, dp % 4
    me1 = x * 2 + core
    me2 = y * 4 + zh * 2 + zl
    me3 = x * 4 + zh * 2 + zl

    loads = [
        pltpu.make_async_copy(cw_hbm, cw, load_sem.at[0]),
        pltpu.make_async_copy(hw_hbm, wt, load_sem.at[1]),
    ] + [
        pltpu.make_async_copy(tg_hbm.at[:, 0, j * Q:(j + 1) * Q], tg.at[:, j * Q:(j + 1) * Q], load_sem.at[2 + j])
        for j in range(4)
    ]
    for cp in loads:
        cp.start()

    def peer1(d):
        slot = lax.rem(me1 + d, 8)
        return slot, (dp, (slot // 2) * 4 + zl * 2 + slot % 2)

    def peer2(d):
        slot = lax.rem(me2 + d, 16)
        return slot, (((slot // 2) % 2) * 4 + slot // 4, x * 4 + (slot % 2) * 2 + core)

    def peerx(d):
        slot = lax.rem(x + d, 4)
        return slot, (dp, slot * 4 + zl * 2 + core)

    def peery(d):
        slot = lax.rem(y + d, 4)
        return slot, (zh * 4 + slot, sq)

    def dev2(i):
        return ((i // 2) % 2) * 4 + i // 4, x * 4 + (i % 2) * 2 + core

    def dev3(i):
        return ((i // 2) % 2) * 4 + y, (i // 4) * 4 + (i % 2) * 2 + core

    def peer3(d):
        slot = lax.rem(me3 + d, 16)
        return slot, dev3(slot)

    barrier = pltpu.get_barrier_semaphore()

    @pl.loop(0, 9)
    def _(i):
        slot = lax.rem(x + 1 + i // 3, 4) * 4 + lax.rem(zh * 2 + zl + 1 + i % 3, 4)
        pl.semaphore_signal(barrier, inc=1, device_id=dev3(slot), device_id_type=MESH)

    @pl.loop(1, 8)
    def _(d):
        pl.semaphore_signal(barrier, inc=1, device_id=peer1(d)[1], device_id_type=MESH)

    @pl.loop(1, 16)
    def _(d):
        pl.semaphore_signal(barrier, inc=1, device_id=peer2(d)[1], device_id_type=MESH)

    def exchange(buf, k, me, count, peer, ssem, rsem, do):
        def cp(d):
            slot, dev = peer(d)
            return slot, dev

        if do == "start":
            @pl.loop(1, count)
            def _(d):
                slot, dev = peer(d)
                pltpu.make_async_remote_copy(
                    src_ref=buf.at[k, me], dst_ref=buf.at[k, me], send_sem=ssem.at[slot], recv_sem=rsem.at[k, me],
                    device_id=dev, device_id_type=MESH,
                ).start()
        else:
            @pl.loop(1, count)
            def _(d):
                slot, dev = peer(d)
                pltpu.make_async_remote_copy(
                    src_ref=buf.at[k, me], dst_ref=buf.at[k, slot], send_sem=ssem.at[slot], recv_sem=rsem.at[k, slot],
                    device_id=dev, device_id_type=MESH,
                ).wait()

    def merge(buf, k, count, each, forward):
        parts = [buf[k, i] for i in range(count)]
        total = functools.reduce(lambda a, b: a + b, parts)
        if not forward:
            return total
        mean = total[0:1] * (1.0 / count)
        dev = functools.reduce(lambda a, b: a + b, [jnp.square(p[0:1] - mean) for p in parts])
        return jnp.concatenate([mean, total[1:2] + each * dev], axis=0)

    def sync(k, value, forward, work1=None, work2=None):
        b1[k, me1] = value
        exchange(b1, k, me1, 8, peer1, s1_sem, r1_sem, "start")
        if work1 is not None:
            work1()
        exchange(b1, k, me1, 8, peer1, s1_sem, r1_sem, "wait")
        b2[k, me2] = merge(b1, k, 8, float(R), forward)
        exchange(b2, k, me2, 16, peer2, s2_sem, r2_sem, "start")
        if work2 is not None:
            work2()
        exchange(b2, k, me2, 16, peer2, s2_sem, r2_sem, "wait")
        return merge(b2, k, 16, float(R * 8), forward)

    def a2a(n, src, dst, do):
        for d in range(1, 4):
            slot, dev = peerx(d)
            mine = pltpu.make_async_remote_copy(
                src_ref=src.at[slot], dst_ref=dst.at[x], send_sem=as_sem.at[n, d], recv_sem=ar_sem.at[n, x],
                device_id=dev, device_id_type=MESH,
            )
            if do == "start":
                mine.start()
            else:
                mine.wait_send()
                pltpu.make_async_remote_copy(
                    src_ref=src.at[slot], dst_ref=dst.at[slot], send_sem=as_sem.at[n, d], recv_sem=ar_sem.at[n, slot],
                    device_id=dev, device_id_type=MESH,
                ).wait_recv()

    def chunks(body, init=None, step=CH):
        def f(i, carry):
            return body(pl.multiple_of(i * step, step), carry)
        return lax.fori_loop(0, R // step, f, init)

    def stats(load):
        zero = jnp.zeros((8, C), F32)
        total = chunks(lambda o, acc: acc + fold(load(o)), zero)
        mean = jnp.sum(total, axis=0, keepdims=True) * (1.0 / R)
        m2 = chunks(lambda o, acc: acc + fold(jnp.square(load(o) - mean)), zero)
        return jnp.concatenate([mean, jnp.sum(m2, axis=0, keepdims=True)], axis=0)

    first = stats(lambda o: seq_ref[pl.ds(o, CH), :].astype(F32))
    tracks = hb_ref.shape[0]

    def prepare_bias():
        hbp[...] = jnp.zeros(hbp.shape, F32)
        last = tracks // Q * Q
        for i in range(tracks // Q):
            hbp[i:i + 1, :] = hb_ref[pl.ds(i * Q, Q)].reshape(1, Q)
        hbp[tracks // Q:tracks // Q + 1, 0:tracks - last] = hb_ref[pl.ds(last, tracks - last)].reshape(1, tracks - last)

        @pl.loop(0, hbp.shape[0] - 6)
        def _(i):
            bcol[pl.ds(pl.multiple_of(i * Q, Q), Q), :] = jnp.broadcast_to(hbp[pl.ds(i, 1), :], (Q, Q)).T

    zeros = jnp.zeros((PAD, C), BF16)
    for buf in (act0, act1, gpad):
        buf[0:PAD] = zeros
        buf[PAD + R:] = zeros
    pl.semaphore_wait(barrier, 31)

    def begin():
        for d in range(1, 4):
            slot, dev = peerx(d)
            pltpu.make_async_remote_copy(
                src_ref=seq_ref.at[pl.ds(pl.multiple_of(slot * Q, Q), Q)], dst_ref=xq.at[x], send_sem=as_sem.at[0, d],
                recv_sem=ar_sem.at[0, x], device_id=dev, device_id_type=MESH,
            ).start()
        xq[x] = seq_ref[pl.ds(pl.multiple_of(x * Q, Q), Q), :]

    def prepare_weights():
        loads[1].wait()
        tracks = wt.shape[0]
        edge = tracks // 256 * 256
        wtail[...] = jnp.zeros(wtail.shape, BF16)
        wtail[0:tracks - edge] = wt[edge:tracks]

        @pl.loop(0, tracks // 256)
        def _(i):
            o = pl.multiple_of(i * 256, 256)
            w[:, pl.ds(o, 256)] = wt[pl.ds(o, 256), :].T
        w[:, edge:edge + 256] = wtail[...].T

    def prepare_counts():
        for cp in loads[2:]:
            cp.wait()
        tracks = tg.shape[0]
        edge = tracks // 256 * 256
        ttail[...] = jnp.zeros(ttail.shape, jnp.int32)
        ttail[0:tracks - edge] = tg[edge:tracks]

    def blocked(ref):
        return lambda o: ref[o // Q, pl.ds(lax.rem(o, Q), CH), :].astype(F32)

    def loader(ref):
        return lambda o: ref[pl.ds(o, CH), :]

    load_x = [blocked(xq), loader(x1), blocked(x2)]
    acts, actTs, gps = [act0, act1, None], [actT0, actT1], [gp0, gp1]
    norms = []

    def norm(k, moments):
        inv = lax.rsqrt(moments[1:2] * (1.0 / (R * NDEV)) + EPS)
        norms.append((moments[0:1], inv, gain_ref[k:k + 1, :], shift_ref[k:k + 1, :]))

    def xhat_at(k, o, load=None):
        mean, inv, _, _ = norms[k]
        return ((load or load_x[k])(o) - mean) * inv

    def pre_at(k, o):
        load = blocked(x2o) if k == 2 else None
        return xhat_at(k, o, load) * norms[k][2] + norms[k][3]

    def activate(k, store):
        def body(o, _):
            pre = pre_at(k, o)
            store(o, (pre * cdf_of(pre)).astype(BF16))
        chunks(body)

    def slopes(k):
        def body(o, _):
            gps[k][pl.ds(o, CH), :] = slope_of(pre_at(k, o))
        chunks(body)

    moments = sync(0, first, True, begin, prepare_weights)
    norm(0, moments)
    a2a(0, xq, xq, "wait")
    loads[0].wait()
    spans = (Q, 2 * Q)
    for l in range(2):
        act, span = acts[l], spans[l]

        def keep(o, v, act=act):
            act[pl.ds(PAD + o, CH), :] = v

        activate(l, keep)
        for r in range(0, R, 256):
            acc = nn(act[pl.ds(PAD - span + r, 256), :], cw[l, 0])
            acc += nn(act[pl.ds(PAD + r, 256), :], cw[l, 1])
            acc += nn(act[pl.ds(PAD + span + r, 256), :], cw[l, 2])
            if l == 0:
                old = jnp.concatenate([xq[r // Q], xq[r // Q + 1]], axis=0).astype(F32)
            else:
                old = x1[pl.ds(r, 256), :]
            new = old + acc
            if l == 0:
                x1[pl.ds(r, 256), :] = new
            else:
                x2[r // Q] = new[0:Q]
                x2[r // Q + 1] = new[Q:2 * Q]

        def side(l=l, act=act):
            if l == 1:
                a2a(1, x2, x2o, "start")
                x2o[x] = x2[x]
            slopes(l)
            actTs[l][...] = act[pl.ds(PAD, R), :].T

        moments = sync(l + 1, stats(load_x[l + 1]), True, side, (prepare_bias, prepare_counts)[l])
        norm(l + 1, moments)

    full = tracks // TW
    rest = tracks - full * TW
    tiles = full + 1
    half = C // 2
    other = (dp, sq + 1 - 2 * core)

    def rcopy(src, dst, ssem, rsem, dev):
        return pltpu.make_async_remote_copy(
            src_ref=src, dst_ref=dst, send_sem=ssem, recv_sem=rsem, device_id=dev, device_id_type=MESH
        )

    def keep_h(o, v):
        h[o // Q, pl.ds(lax.rem(o, Q), CH), :] = v

    a2a(1, x2, x2o, "wait")
    activate(2, keep_h)
    for k in range(4):
        part = h[k].T
        hT[:, k * Q:(k + 1) * Q] = part
        wide = part.astype(F32)
        for s in range(16):
            sx, sz, sc = s // 4, (s // 2) % 2, s % 2
            to = jnp.where(core == sc, half, 0) + sx * 48 + sz * 24
            dhacc[pl.ds(pl.multiple_of(to, 8), 24), k * Q:(k + 1) * Q] = wide[24 * s:24 * s + 24]
    hPb[0:C] = dhacc[...].astype(BF16)
    ones_row = lax.broadcasted_iota(jnp.int32, (16, R), 0) == 0
    hPb[C:C + 16] = jnp.where(ones_row, 1.0, 0.0).astype(BF16)
    scale = 1.0 / math.sqrt(R * NDEV)

    def piece(rows, counts, bias, at, live):
        v = nn(rows, hT[...])
        for j in range(4):
            z = v[:, j * Q:(j + 1) * Q] + bias
            e = (jnp.exp(z) - counts[:, j * Q:(j + 1) * Q].astype(F32)) * scale
            if live is not None:
                e = jnp.where(lax.broadcasted_iota(jnp.int32, e.shape, 0) < live, e, 0.0)
            dz[at:at + 256, j * Q:(j + 1) * Q] = e.astype(BF16)

    def tile(t, start, tail, turn):
        for i in range(3):
            o = start + i * 256 if tail else pl.multiple_of(start + i * 256, 256)
            if tail and i == 2:
                piece(wtail[...], ttail[...], bcol[pl.ds(o, 256), :], i * 256, rest - 512)
            else:
                piece(wt[pl.ds(o, 256), :], tg[pl.ds(o, 256), :], bcol[pl.ds(o, 256), :], i * 256, None)
        part = nt(hPb[...], dz[...])
        gsend[t] = part[0:half].astype(BF16)
        gown[turn] = part[half:C]
        bb1[0, me1, pl.ds(t, 1), :] = part[C:C + 1]
        add = nn(w[:, pl.ds(start if tail else pl.multiple_of(start, TW), TW)], dz[...])
        dhacc[...] += add
        rcopy(gsend.at[t], grecv.at[t], gcs.at[t], gcr.at[t], other).start()

    def chip(t, slot):
        rcopy(gsend.at[t], grecv.at[t], gcs.at[t], gcr.at[t], other).wait()
        for k in range(4):
            xsend[t, k] = (gown[slot, k * 48:(k + 1) * 48] + grecv[t, k * 48:(k + 1) * 48].astype(F32)).astype(BF16)

    def xstart(t):
        for d in range(1, 4):
            slot, dev = peerx(d)
            rcopy(xsend.at[t, slot], xrecv.at[t, x], gxs.at[t, slot], gxr.at[t, x], dev).start()

    def owner(t, i):
        return t, x * 4 + i * 2 + core

    def yz(t, i):
        return rcopy(ysend.at[t, i], yrecv.at[me2], gys.at[t, i], gyr.at[me2], owner(t, i))

    def spread_rows(t, total):
        for i in range(2):
            ysend[t, i] = total[i * 24:i * 24 + 24].astype(BF16)

            @pl.when(jnp.logical_or(dp != t, zl != i))
            def _(i=i):
                yz(t, i).start()

    def ystart(t):
        total = xsend[t, x].astype(F32)
        for d in range(1, 4):
            slot, dev = peerx(d)
            rcopy(xsend.at[t, slot], xrecv.at[t, slot], gxs.at[t, slot], gxr.at[t, slot], dev).wait()
            total = total + xrecv[t, slot].astype(F32)
        spread_rows(t, total)

    def vstart(t):
        @pl.when(y != t)
        def _():
            rcopy(xsend.at[t], vrecv.at[y], hvs.at[t], hvr.at[y], (zh * 4 + t, sq)).start()

    def vmid():
        for d in range(1, 4):
            slot, dev = peery(d)
            rcopy(vrecv.at[slot], vrecv.at[slot], hvs.at[slot], hvr.at[slot], dev).wait_recv()
        for k in range(4):
            total = xsend[y, k].astype(F32)
            for d in range(1, 4):
                total = total + vrecv[lax.rem(y + d, 4), k].astype(F32)
            vsend[k] = total.astype(BF16)
        for d in range(1, 4):
            slot, dev = peerx(d)
            rcopy(vsend.at[slot], vx.at[x], hxs.at[slot], hxr.at[x], dev).start()

    def vend():
        total = vsend[x].astype(F32)
        for d in range(1, 4):
            slot, dev = peerx(d)
            rcopy(vsend.at[slot], vx.at[slot], hxs.at[slot], hxr.at[slot], dev).wait()
            total = total + vx[slot].astype(F32)
        spread_rows(y, total)
        for d in range(1, 4):
            slot, dev = peery(d)
            rcopy(xsend.at[slot], vrecv.at[slot], hvs.at[slot], hvr.at[slot], dev).wait_send()

    def finish_head():
        @pl.when(dp < tiles)
        def _():
            near = dp < 4

            def body(d, total):
                slot = jnp.where(near, y * 4 + lax.rem(me2 + d, 4), lax.rem(me2 + d, 16))
                rcopy(yrecv.at[slot], yrecv.at[slot], gys.at[0, 0], gyr.at[slot], dev2(slot)).wait_recv()
                return total + yrecv[slot].astype(F32)
            total = lax.fori_loop(1, jnp.where(near, 4, 16), body, ysend[dp, zl].astype(F32))
            fall[dp] = total.astype(BF16)

            @pl.loop(1, 8)
            def _(d):
                slot = lax.rem(dp + d, 8)
                rcopy(fall.at[dp], fall.at[dp], gfs.at[slot], gfr.at[dp], (slot, sq)).start()

    def collect_head():
        @pl.loop(0, tiles)
        def _(t):
          @pl.when(jnp.logical_or(t >= 4, t == y))
          def _():
            for i in range(2):
                @pl.when(jnp.logical_or(dp != t, zl != i))
                def _(i=i):
                    yz(t, i).wait_send()

        @pl.when(dp < tiles)
        def _():
            @pl.loop(1, 8)
            def _(d):
                slot = lax.rem(dp + d, 8)
                rcopy(fall.at[dp], fall.at[dp], gfs.at[slot], gfr.at[dp], (slot, sq)).wait_send()

        for t in range(tiles):
            @pl.when(dp != t)
            def _(t=t):
                rcopy(fall.at[t], fall.at[t], gfs.at[0], gfr.at[t], (t, sq)).wait_recv()
        for t in range(full):
            ghead_ref[:, t * TW:(t + 1) * TW] = fall[t].astype(F32)
        ghead_ref[:, full * TW:tracks] = fall[full].astype(F32)[:, 0:rest]

    def bias_start():
        exchange(bb1, 0, me1, 8, peer1, e1_sem, q1_sem, "start")

    def bias_middle():
        exchange(bb1, 0, me1, 8, peer1, e1_sem, q1_sem, "wait")
        bb2[0, me2] = functools.reduce(lambda a, b: a + b, [bb1[0, i] for i in range(8)])
        exchange(bb2, 0, me2, 16, peer2, e2_sem, q2_sem, "start")

    def bias_end():
        exchange(bb2, 0, me2, 16, peer2, e2_sem, q2_sem, "wait")
        total = functools.reduce(lambda a, b: a + b, [bb2[0, i] for i in range(16)])
        for t in range(tiles):
            n = min(TW, tracks - t * TW)
            gbias_ref[pl.ds(t * TW, n)] = total[t, 0:n]

    bb1[0, me1] = jnp.zeros((8, TW), F32)
    dhacc[...] = jnp.zeros(dhacc.shape, F32)

    def near(i):
        return lax.rem(y + 1 + i, 4)

    @pl.loop(0, 3)
    def _(i):
        tile(near(i), near(i) * TW, False, i % 2)

        @pl.when(i > 0)
        def _():
            chip(near(i - 1), (i + 1) % 2)
            vstart(near(i - 1))

    tile(full, full * TW, True, 1)
    chip(near(2), 0)
    vstart(near(2))

    @pl.loop(0, 3)
    def _(i):
        t = jnp.where(i == 0, 4, jnp.where(i == 1, y, 5))
        tile(t, t * TW, False, i % 2)
        chip(jnp.where(i == 0, full, jnp.where(i == 1, 4, y)), (i + 1) % 2)

        @pl.when(i == 0)
        def _():
            xstart(full)

    chip(5, 0)

    class Job:
        def __init__(self, number, layer, taps, at, ring, me, peer, dev):
            self.q, self.layer, self.taps, self.at, self.ring = number, layer, taps, at, ring
            self.me, self.peer, self.dev, self.owners = me, peer, dev, 3 * len(taps)

    jobs = (
        Job(0, 1, (0, 1, 2), y, peery, me3, peer3, dev3),
        Job(1, 0, (0, 2), x, peerx, me2, peer2, dev2),
        Job(2, 0, (1,), y, peery, me3, peer3, dev3),
    )

    def conv_start(l, span, actT, taps):
        for j in taps:
            cfull[j] = nn(actT[...], gpad[pl.ds(PAD + (1 - j) * span, R), :])
            csend[l, j] = cfull[j, pl.ds(pl.multiple_of((1 - core) * half, 64), half), :].astype(BF16)
            rcopy(csend.at[l, j], crecv.at[l, j], ccs.at[l, j], ccr.at[l, j], other).start()

    def conv_x(job):
        l, q = job.layer, job.q
        for i, j in enumerate(job.taps):
            rcopy(csend.at[l, j], crecv.at[l, j], ccs.at[l, j], ccr.at[l, j], other).wait()
            for k in range(4):
                mine = cfull[j, pl.ds(pl.multiple_of(core * half + k * 48, 16), 48), :]
                cx[q, i, k] = (mine + crecv[l, j, k * 48:(k + 1) * 48].astype(F32)).astype(BF16)
            for d in range(1, 4):
                slot, dev = job.ring(d)
                rcopy(cx.at[q, i, slot], cxr.at[q, i, job.at], cxs.at[q, i, slot], cxrs.at[q, i, job.at], dev).start()

    def block(job, i):
        q, me = job.q, job.me
        return rcopy(cy.at[q, i], cyr.at[q, me], cys.at[q, i], cyrs.at[q, me], job.dev(i))

    def conv_rs(job):
        q = job.q
        for j in range(len(job.taps)):
            total = cx[q, j, job.at].astype(F32)
            for d in range(1, 4):
                slot, dev = job.ring(d)
                rcopy(cx.at[q, j, slot], cxr.at[q, j, slot], cxs.at[q, j, slot], cxrs.at[q, j, slot], dev).wait()
                total = total + cxr[q, j, slot].astype(F32)
            for b in range(3):
                i = 3 * j + b
                cy[q, i] = total[b * 16:(b + 1) * 16].astype(BF16)

                @pl.when(job.me != i)
                def _(i=i):
                    block(job, i).start()

    def piece_of(job):
        return cz.at[job.q, job.me // 3, job.me % 3]

    def conv_ag(job):
        q = job.q

        @pl.when(job.me < job.owners)
        def _():
            def body(d, total):
                slot, dev = job.peer(d)
                rcopy(cyr.at[q, slot], cyr.at[q, slot], cys.at[q, 0], cyrs.at[q, slot], dev).wait_recv()
                return total + cyr[q, slot].astype(F32)
            total = lax.fori_loop(1, 16, body, cy[q, job.me].astype(F32))
            cz[q, job.me // 3, job.me % 3] = total.astype(BF16)

            @pl.loop(1, 16)
            def _(d):
                slot, dev = job.peer(d)
                rcopy(piece_of(job), piece_of(job), czs.at[q, slot], czrs.at[q, job.me], dev).start()

    def conv_xag(job):
        q = job.q
        for j in range(len(job.taps)):
            for b in range(3):
                i = 3 * j + b

                @pl.when(job.me != i)
                def _(i=i, j=j, b=b):
                    rcopy(cz.at[q, j, b], cz.at[q, j, b], czs.at[q, 0], czrs.at[q, i], job.dev(i)).wait_recv()
            for d in range(1, 4):
                slot, dev = job.ring(d)
                rcopy(cz.at[q, j], ca.at[q, j, job.at], cas.at[q, j, slot], cars.at[q, j, job.at], dev).start()
            ca[q, j, job.at] = cz[q, j]

    def conv_cag(job):
        q = job.q
        for i, j in enumerate(job.taps):
            for d in range(1, 4):
                slot, dev = job.ring(d)
                rcopy(cz.at[q, i], ca.at[q, i, slot], cas.at[q, i, slot], cars.at[q, i, slot], dev).wait()
            rcopy(ca.at[q, i], cb.at[q, i], cbs.at[q, i], cbrs.at[q, i], other).start()
            gconv_ref[job.layer, j, core] = ca[q, i]

    def conv_end(job):
        q = job.q
        for i, j in enumerate(job.taps):
            rcopy(ca.at[q, i], cb.at[q, i], cbs.at[q, i], cbrs.at[q, i], other).wait()
            gconv_ref[job.layer, j, 1 - core] = cb[q, i]
        for i in range(job.owners):
            @pl.when(job.me != i)
            def _(i=i):
                block(job, i).wait_send()

        @pl.when(job.me < job.owners)
        def _():
            @pl.loop(1, 16)
            def _(d):
                slot, dev = job.peer(d)
                rcopy(piece_of(job), piece_of(job), czs.at[q, slot], czrs.at[q, job.me], dev).wait_send()

    n = float(R * NDEV)

    def sums(k, load):
        def body(o, acc):
            v = load(o) * gps[k][pl.ds(o, CH), :]
            dpre[pl.ds(o, CH), :] = v
            return acc[0] + fold(v), acc[1] + fold(v * xhat_at(k, o))
        zero = jnp.zeros((8, C), F32)
        a, b = chunks(body, (zero, zero))
        return jnp.concatenate([jnp.sum(a, axis=0, keepdims=True), jnp.sum(b, axis=0, keepdims=True)], axis=0)

    def report(k, s):
        gshift_ref[k:k + 1, :] = s[0:1]
        ggain_ref[k:k + 1, :] = s[1:2]

    def dv_at(k, o, s):
        _, inv, gain, _ = norms[k]
        v = blocked(dpq)(o) if k == 2 else dpre[pl.ds(o, CH), :]
        return gain * inv * (v - s[0:1] * (1.0 / n) - xhat_at(k, o) * (s[1:2] * (1.0 / n)))

    def back(o, acc):
        k = o // Q
        v = dpre[pl.ds(o, CH), :] * slope_of(pre_at(2, o))
        dps[k, pl.ds(lax.rem(o, Q), CH), :] = v.astype(BF16)
        return acc[0] + fold(v), acc[1] + fold(v * xhat_at(2, o, blocked(x2o)))

    for k in range(4):
        dpre[k * Q:(k + 1) * Q] = dhacc[:, k * Q:(k + 1) * Q].T
    zero = jnp.zeros((8, C), F32)
    left, right = chunks(back, (zero, zero))
    value = jnp.concatenate([jnp.sum(left, axis=0, keepdims=True), jnp.sum(right, axis=0, keepdims=True)], axis=0)

    def fill31():
        bias_start()
        a2a(2, dps, dpq, "start")
        dpq[x] = dps[x]
        xstart(4)
        xstart(5)

    def fill32():
        bias_middle()
        ystart(full)

    s = sync(3, value, False, fill31, fill32)
    report(2, s)
    a2a(2, dps, dpq, "wait")

    for l in (1, 0):
        span = spans[l]

        def spread(o, _, l=l, s=s):
            v = dv_at(l + 1, o, s)
            if l == 0:
                v = v + g[pl.ds(o, CH), :]
            g[pl.ds(o, CH), :] = v
            gpad[pl.ds(PAD + o, CH), :] = v.astype(BF16)

        chunks(spread)
        if l == 0:
            conv_start(0, span, actTs[0], (0, 1, 2))
        for r in range(0, R, 256):
            acc = nt(gpad[pl.ds(PAD + span + r, 256), :], cw[l, 0])
            acc += nt(gpad[pl.ds(PAD + r, 256), :], cw[l, 1])
            acc += nt(gpad[pl.ds(PAD - span + r, 256), :], cw[l, 2])
            dpre[pl.ds(r, 256), :] = acc

        if l == 0:
            conv_x(jobs[1])
            conv_x(jobs[2])
        value = sums(l, lambda o: dpre[pl.ds(o, CH), :])

        def early(l=l, span=span):
            if l == 0:
                conv_ag(jobs[0])
                _, inv, gain, _ = norms[0]

                def body(o, _):
                    v = g[pl.ds(o, CH), :] + gain * inv * dpre[pl.ds(o, CH), :]
                    asend[o // Q, pl.ds(lax.rem(o, Q), CH), :] = v.astype(BF16)
                chunks(body)
                a2a(3, asend, arecv, "start")
                arecv[x] = asend[x]
                conv_rs(jobs[2])
                conv_rs(jobs[1])
            else:
                conv_start(1, span, actTs[1], (0, 1, 2))
                vmid()
                conv_x(jobs[0])

        def late(l=l):
            if l == 1:
                ystart(4)
                ystart(5)
                vend()
                conv_rs(jobs[0])
            else:
                conv_xag(jobs[0])
                conv_ag(jobs[2])
                conv_ag(jobs[1])

        s = sync(5 - l, value, False, early, late)
        report(l, s)

    a2a(3, asend, arecv, "wait")
    mean, inv, gain, _ = norms[0]

    def finish(o, _):
        xh = (seq_ref[pl.ds(o, CH), :].astype(F32) - mean) * inv
        part = blocked(arecv)(o)
        gin_ref[pl.ds(o, CH), :] = part - gain * inv * (s[0:1] * (1.0 / n) + xh * (s[1:2] * (1.0 / n)))
    chunks(finish)
    conv_xag(jobs[2])
    conv_xag(jobs[1])
    finish_head()
    conv_cag(jobs[0])
    bias_end()
    conv_cag(jobs[2])
    conv_cag(jobs[1])
    conv_end(jobs[0])
    collect_head()
    conv_end(jobs[2])
    conv_end(jobs[1])


def emit(gin, ggain, gshift, ghead, gbias, gconv, *rest):
    outs, bufs, wide, isem, osem = rest[:6], rest[6:12], rest[12], rest[13], rest[14]
    ins = [pltpu.make_async_copy(src, dst, isem.at[i]) for i, (src, dst) in
           enumerate(zip((gin, ggain, gshift, ghead, gbias), bufs))]
    taps = [pltpu.make_async_copy(gconv.at[j], bufs[5].at[j], isem.at[5 + j]) for j in range(6)]
    for cp in taps + ins:
        cp.start()
    back = [pltpu.make_async_copy(src, dst, osem.at[i]) for i, (src, dst) in
            enumerate(zip(bufs, (outs[0], outs[2], outs[3], outs[4], outs[5])))]
    send = [pltpu.make_async_copy(wide.at[j], outs[1].at[j], osem.at[5 + j]) for j in range(6)]
    for j in range(6):
        taps[j].wait()
        wide[j] = bufs[5][j].astype(F32)
        send[j].start()
    for a, b in zip(ins, back):
        a.wait()
        b.start()
    for cp in send + back:
        cp.wait()


def on_device(sequence, conv_weight, gains, shifts, head_weight, head_bias, targets):
    tracks = head_weight.shape[1]
    vmem = pl.BlockSpec(memory_space=pltpu.VMEM)
    hbm = pl.BlockSpec(memory_space=pl.ANY)
    sds = jax.ShapeDtypeStruct
    V = pltpu.VMEM
    D = pltpu.SemaphoreType.DMA
    T7 = tracks // TW + 1
    W7 = T7 * TW
    gin, ggain, gshift, ghead, gbias, gconv = pl.pallas_call(
        kernel,
        out_shape=(
            sds((R, C), F32), sds((3, C), F32), sds((3, C), F32), sds((C // 16, tracks), F32), sds((tracks,), F32),
            sds((2, 3, 2, 4, 3, 16, C), BF16),
        ),
        in_specs=[vmem, vmem, vmem, vmem, hbm, hbm, hbm],
        out_specs=(vmem,) * 6,
        scratch_shapes=[
            V((2, 3, C, C), BF16), V((tracks, C), BF16), V((256, C), BF16), V((C, W7), BF16),
            V((tracks, R), jnp.int32), V((256, R), jnp.int32), V((W7, Q), F32), V((48, Q), F32),
            V((4, Q, C), BF16), V((R, C), F32), V((4, Q, C), F32), V((4, Q, C), F32),
            V((R + 2 * PAD, C), BF16), V((R + 2 * PAD, C), BF16), V((C, R), BF16), V((C, R), BF16),
            V((C, R), BF16), V((C + 16, R), BF16), V((TW, R), BF16),
            V((C, R), F32), V((4, Q, C), BF16), V((4, Q, C), BF16),
            V((R, C), F32), V((R, C), F32), V((R + 2 * PAD, C), BF16), V((R, C), F32), V((R, C), F32),
            V((4, Q, C), BF16),
            V((6, 8, 2, C), F32), V((6, 16, 2, C), F32), V((1, 8, 8, TW), F32), V((1, 16, 8, TW), F32),
            V((T7, 192, TW), BF16), V((T7, 192, TW), BF16), V((2, 192, TW), F32),
            V((T7, 4, 48, TW), BF16), V((T7, 4, 48, TW), BF16), V((T7, 2, 24, TW), BF16), V((16, 24, TW), BF16), V((T7, 24, TW), BF16),
            V((4, 4, 48, TW), BF16), V((4, 48, TW), BF16), V((4, 48, TW), BF16),
            V((3, C, C), F32), V((2, 3, C // 2, C), BF16), V((2, 3, C // 2, C), BF16), V((3, 3, 4, 48, C), BF16),
            V((3, 3, 4, 48, C), BF16), V((3, 9, 16, C), BF16), V((3, 16, 16, C), BF16), V((3, 3, 3, 16, C), BF16),
            V((3, 3, 4, 3, 16, C), BF16), V((3, 3, 4, 3, 16, C), BF16),
            D((6,)), D((8,)), D((16,)), D((6, 8)), D((6, 16)), D((4, 4)), D((4, 4)),
            D((8,)), D((16,)), D((1, 8)), D((1, 16)), D((T7,)), D((T7,)), D((T7, 4)), D((T7, 4)), D((T7, 2)), D((16,)),
            D((8,)), D((T7,)), D((4,)), D((4,)), D((4,)), D((4,)),
            D((2, 3)), D((2, 3)), D((3, 3, 4)), D((3, 3, 4)), D((3, 9)), D((3, 16)), D((3, 16)), D((3, 9)), D((3, 3, 4)), D((3, 3, 4)),
            D((3, 3)), D((3, 3)),
        ],
        compiler_params=pltpu.CompilerParams(
            collective_id=0, has_side_effects=True, vmem_limit_bytes=67043328
        ),
        name="whole",
    )(sequence.reshape(R, C), gains, shifts, head_bias, conv_weight, head_weight.T, jnp.transpose(targets, (2, 0, 1)))
    gin, grad_conv, ggain, gshift, ghead, gbias = pl.pallas_call(
        emit,
        out_shape=(
            sds((R, C), F32), sds((6, C, C), F32), sds((3, C), F32), sds((3, C), F32), sds((C // 16, tracks), F32),
            sds((tracks,), F32),
        ),
        in_specs=[hbm] * 6,
        out_specs=(hbm,) * 6,
        scratch_shapes=[
            V((R, C), F32), V((3, C), F32), V((3, C), F32), V((C // 16, tracks), F32), V((tracks,), F32),
            V((6, C, C), BF16), V((6, C, C), F32), D((11,)), D((11,)),
        ],
        name="emit",
    )(gin, ggain, gshift, ghead, gbias, gconv.reshape(6, C, C))
    return gin.reshape(1, R, C), grad_conv.reshape(2, 3, C, C), ggain, gshift, ghead, gbias


def solution(mesh):
    rep = P()
    return jax.shard_map(
        on_device,
        mesh=mesh,
        in_specs=(P("dp", "seq", None), rep, rep, rep, rep, rep, P("dp", "seq", None)),
        out_specs=(P("dp", "seq", None), rep, rep, rep, P("seq", None), rep),
        check_vma=False,
    )
```

time: 146 us -> 121 us (0.83)
  Pallas kernels: 135 us -> 119 us
  local copies, waits for them, and re-layouts: 4.31 us -> 0 us
  other arithmetic: 3.52 us -> 0 us
    pallas_call x1, Pallas kernels: 135 us -> 116 us  [on_device(): pl.pallas_call(kernel, out_shape=(sds((R, C), F32), sds((3, C), F32), sds...]
    convert_element_type x1 -> x0, other arithmetic: 3.52 us -> none  [on_device(): grad_conv = gconv.reshape(2, 3, C, C).astype(F32)]
    pallas_call x0 -> x1, Pallas kernels: none -> 3.41 us  [on_device(): pl.pallas_call(emit, out_shape=(sds((R, C), F32), sds((6, C, C), F32), sd...]
    unnamed x12 -> x0, local copies, waits for them, and re-layouts: 2.87 us -> none
where the time goes in v3:
time: 121 us; the launch traced here: 120 us
  Pallas kernels  119 us (98%)
    pallas_call x1, Pallas kernels, on_device(): pl.pallas_call(kernel, out_shape=(sds((R, C), F32), sds((3, C), F32), sds...  116 us
    pallas_call x1, Pallas kernels, on_device(): pl.pallas_call(emit, out_shape=(sds((R, C), F32), sds((6, C, C), F32), sd...  3.41 us

profile of v3, /device:TPU:0, one launch (start us, length us, event | category | flops | bytes accessed | tf_op | source)
XLA Modules:
  0.0 119.9 jit_solution(9687067860186813551)
XLA Ops:
  0.6 115.7 %whole.1 = (f32[512,384]{1,0:T(8,128)}, f32[3,384]{1,0:T(4,128)}, f32[3,384]{1,0:T(4,128)}, f32[24,5313]{1,0:T(8,128)}, f32[5313]{0:T(1024)}, /*index=5*/bf16[2,3,2,4,3,16,384]{6,5,4,3,2,1,0:T(8,128)(2,1)}) custom-call(bf16[512,384]{1,0:T(8,128)(2,1)} %bitcast.9, f32[3,384]{1,0:T(4,128)} %gain_ref.1, f32[3,384]{1,0:T(4,128)} %shift_ref.1, f32[5313]{0:T(1024)} %hb_ref.1, ...), custom_call_target="tpu_custom_call" | custom-call | tf_op jit(solution)/shard_map/whole/pallas_call | solution.py:771
  116.3 3.4 %emit.1 = (f32[512,384]{1,0:T(8,128)}, f32[6,384,384]{2,1,0:T(8,128)}, f32[3,384]{1,0:T(4,128)}, f32[3,384]{1,0:T(4,128)}, f32[24,5313]{1,0:T(8,128)}, /*index=5*/f32[5313]{0:T(1024)}) custom-call(f32[512,384]{1,0:T(8,128)} %get-tuple-element.18.gin, f32[3,384]{1,0:T(4,128)} %get-tuple-element.19.ggain, f32[3,384]{1,0:T(4,128)} %get-tuple-element.20.gshift, ...), custom_call_target="tpu_custom_call" | custom-call | tf_op jit(solution)/shard_map/emit/pallas_call | solution.py:806

commit v4 on v3

--- a/solution.py
+++ b/solution.py
@@ -42,15 +42,16 @@
 
 
 def kernel(
-    seq_ref, gain_ref, shift_ref, hb_ref, cw_hbm, hw_hbm, tg_hbm,
-    gin_ref, ggain_ref, gshift_ref, ghead_ref, gbias_ref, gconv_ref,
+    seq_hbm, gain_hbm, shift_hbm, hb_hbm, cw_hbm, hw_hbm, tg_hbm,
+    gin_hbm, ggain_ref, gshift_ref, ghead_hbm, gbias_ref, gconv_hbm,
+    seq_ref, gain_ref, shift_ref, hb_ref, ghead_ref,
     cw, wt, wtail, w, tg, ttail, bcol, hbp, xq, x1, x2, x2o, act0, act1, actT0, actT1, hT, hPb, dz, dhacc, dps, dpq,
-    gp0, gp1, gpad, g, dpre, arecv, b1, b2, bb1, bb2,
+    gp0, gp1, gpad, g, dpre, arecv, b1, b2, bb1, brow, bin_, ball,
     gsend, grecv, gown, xsend, xrecv, ysend, yrecv, fall, vrecv, vsend, vx,
     cfull, csend, crecv, cx, cxr, cy, cyr, cz, ca, cb,
     load_sem, s1_sem, s2_sem, r1_sem, r2_sem, as_sem, ar_sem,
-    e1_sem, e2_sem, q1_sem, q2_sem, gcs, gcr, gxs, gxr, gys, gyr, gfs, gfr, hvs, hvr, hxs, hxr,
-    ccs, ccr, cxs, cxrs, cys, cyrs, czs, czrs, cas, cars, cbs, cbrs,
+    e1_sem, e2_sem, q1_sem, q2_sem, brs, brr, gcs, gcr, gxs, gxr, gys, gyr, gfs, gfr, hvs, hvr, hxs, hxr,
+    out_sem, oc_sem, ccs, ccr, cxs, cxrs, cys, cyrs, czs, czrs, cas, cars, cbs, cbrs,
 ):
     h = asend = dps
     dp = lax.axis_index("dp")
@@ -61,6 +62,51 @@
     me2 = y * 4 + zh * 2 + zl
     me3 = x * 4 + zh * 2 + zl
 
+    def peer1(d):
+        slot = lax.rem(me1 + d, 8)
+        return slot, (dp, (slot // 2) * 4 + zl * 2 + slot % 2)
+
+    def peer2(d):
+        slot = lax.rem(me2 + d, 16)
+        return slot, (((slot // 2) % 2) * 4 + slot // 4, x * 4 + (slot % 2) * 2 + core)
+
+    def peerx(d):
+        slot = lax.rem(x + d, 4)
+        return slot, (dp, slot * 4 + zl * 2 + core)
+
+    def peery(d):
+        slot = lax.rem(y + d, 4)
+        return slot, (zh * 4 + slot, sq)
+
+    def dev2(i):
+        return ((i // 2) % 2) * 4 + i // 4, x * 4 + (i % 2) * 2 + core
+
+    def dev3(i):
+        return ((i // 2) % 2) * 4 + y, (i // 4) * 4 + (i % 2) * 2 + core
+
+    def peer3(d):
+        slot = lax.rem(me3 + d, 16)
+        return slot, dev3(slot)
+
+    barrier = pltpu.get_barrier_semaphore()
+
+    @pl.loop(0, 9)
+    def _(i):
+        slot = lax.rem(x + 1 + i // 3, 4) * 4 + lax.rem(zh * 2 + zl + 1 + i % 3, 4)
+        pl.semaphore_signal(barrier, inc=1, device_id=dev3(slot), device_id_type=MESH)
+
+    @pl.loop(1, 8)
+    def _(d):
+        pl.semaphore_signal(barrier, inc=1, device_id=peer1(d)[1], device_id_type=MESH)
+
+    @pl.loop(1, 16)
+    def _(d):
+        pl.semaphore_signal(barrier, inc=1, device_id=peer2(d)[1], device_id_type=MESH)
+
+    small = [
+        pltpu.make_async_copy(src, dst, load_sem.at[6 + i])
+        for i, (src, dst) in enumerate(((seq_hbm, seq_ref), (gain_hbm, gain_ref), (shift_hbm, shift_ref), (hb_hbm, hb_ref)))
+    ]
     loads = [
         pltpu.make_async_copy(cw_hbm, cw, load_sem.at[0]),
         pltpu.make_async_copy(hw_hbm, wt, load_sem.at[1]),
@@ -68,49 +114,8 @@
         pltpu.make_async_copy(tg_hbm.at[:, 0, j * Q:(j + 1) * Q], tg.at[:, j * Q:(j + 1) * Q], load_sem.at[2 + j])
         for j in range(4)
     ]
-    for cp in loads:
+    for cp in small + loads:
         cp.start()
-
-    def peer1(d):
-        slot = lax.rem(me1 + d, 8)
-        return slot, (dp, (slot // 2) * 4 + zl * 2 + slot % 2)
-
-    def peer2(d):
-        slot = lax.rem(me2 + d, 16)
-        return slot, (((slot // 2) % 2) * 4 + slot // 4, x * 4 + (slot % 2) * 2 + core)
-
-    def peerx(d):
-        slot = lax.rem(x + d, 4)
-        return slot, (dp, slot * 4 + zl * 2 + core)
-
-    def peery(d):
-        slot = lax.rem(y + d, 4)
-        return slot, (zh * 4 + slot, sq)
-
-    def dev2(i):
-        return ((i // 2) % 2) * 4 + i // 4, x * 4 + (i % 2) * 2 + core
-
-    def dev3(i):
-        return ((i // 2) % 2) * 4 + y, (i // 4) * 4 + (i % 2) * 2 + core
-
-    def peer3(d):
-        slot = lax.rem(me3 + d, 16)
-        return slot, dev3(slot)
-
-    barrier = pltpu.get_barrier_semaphore()
-
-    @pl.loop(0, 9)
-    def _(i):
-        slot = lax.rem(x + 1 + i // 3, 4) * 4 + lax.rem(zh * 2 + zl + 1 + i % 3, 4)
-        pl.semaphore_signal(barrier, inc=1, device_id=dev3(slot), device_id_type=MESH)
-
-    @pl.loop(1, 8)
-    def _(d):
-        pl.semaphore_signal(barrier, inc=1, device_id=peer1(d)[1], device_id_type=MESH)
-
-    @pl.loop(1, 16)
-    def _(d):
-        pl.semaphore_signal(barrier, inc=1, device_id=peer2(d)[1], device_id_type=MESH)
 
     def exchange(buf, k, me, count, peer, ssem, rsem, do):
         def cp(d):
@@ -184,10 +189,12 @@
         m2 = chunks(lambda o, acc: acc + fold(jnp.square(load(o) - mean)), zero)
         return jnp.concatenate([mean, jnp.sum(m2, axis=0, keepdims=True)], axis=0)
 
+    small[0].wait()
     first = stats(lambda o: seq_ref[pl.ds(o, CH), :].astype(F32))
     tracks = hb_ref.shape[0]
 
     def prepare_bias():
+        small[3].wait()
         hbp[...] = jnp.zeros(hbp.shape, F32)
         last = tracks // Q * Q
         for i in range(tracks // Q):
@@ -268,6 +275,8 @@
         chunks(body)
 
     moments = sync(0, first, True, begin, prepare_weights)
+    small[1].wait()
+    small[2].wait()
     norm(0, moments)
     a2a(0, xq, xq, "wait")
     loads[0].wait()
@@ -459,23 +468,55 @@
         for t in range(full):
             ghead_ref[:, t * TW:(t + 1) * TW] = fall[t].astype(F32)
         ghead_ref[:, full * TW:tracks] = fall[full].astype(F32)[:, 0:rest]
+        pltpu.make_async_copy(ghead_ref, ghead_hbm, out_sem.at[1]).start()
 
     def bias_start():
         exchange(bb1, 0, me1, 8, peer1, e1_sem, q1_sem, "start")
 
+    def bias_row(t):
+        return rcopy(brow.at[t], bin_.at[me2], brs.at[t], brr.at[me2], dev2(t))
+
     def bias_middle():
         exchange(bb1, 0, me1, 8, peer1, e1_sem, q1_sem, "wait")
-        bb2[0, me2] = functools.reduce(lambda a, b: a + b, [bb1[0, i] for i in range(8)])
-        exchange(bb2, 0, me2, 16, peer2, e2_sem, q2_sem, "start")
+        total = functools.reduce(lambda a, b: a + b, [bb1[0, i] for i in range(8)])
+        for t in range(tiles):
+            brow[t] = total[t:t + 1]
+
+            @pl.when(me2 != t)
+            def _(t=t):
+                bias_row(t).start()
+
+    def bias_own():
+        @pl.when(me2 < tiles)
+        def _():
+            def body(d, total):
+                slot, dev = peer2(d)
+                rcopy(bin_.at[slot], bin_.at[slot], brs.at[0], brr.at[slot], dev).wait_recv()
+                return total + bin_[slot]
+            ball[me2] = lax.fori_loop(1, 16, body, brow[me2])
+
+            @pl.loop(1, 16)
+            def _(d):
+                slot, dev = peer2(d)
+                rcopy(ball.at[me2], ball.at[me2], e2_sem.at[slot], q2_sem.at[me2], dev).start()
 
     def bias_end():
-        exchange(bb2, 0, me2, 16, peer2, e2_sem, q2_sem, "wait")
-        total = functools.reduce(lambda a, b: a + b, [bb2[0, i] for i in range(16)])
         for t in range(tiles):
             n = min(TW, tracks - t * TW)
-            gbias_ref[pl.ds(t * TW, n)] = total[t, 0:n]
-
-    bb1[0, me1] = jnp.zeros((8, TW), F32)
+
+            @pl.when(me2 != t)
+            def _(t=t):
+                bias_row(t).wait_send()
+                rcopy(ball.at[t], ball.at[t], e2_sem.at[0], q2_sem.at[t], dev2(t)).wait_recv()
+            gbias_ref[pl.ds(t * TW, n)] = ball[t][0, 0:n]
+
+        @pl.when(me2 < tiles)
+        def _():
+            @pl.loop(1, 16)
+            def _(d):
+                slot, dev = peer2(d)
+                rcopy(ball.at[me2], ball.at[me2], e2_sem.at[slot], q2_sem.at[me2], dev).wait_send()
+
     dhacc[...] = jnp.zeros(dhacc.shape, F32)
 
     def near(i):
@@ -588,6 +629,11 @@
                 rcopy(cz.at[q, j], ca.at[q, j, job.at], cas.at[q, j, slot], cars.at[q, j, job.at], dev).start()
             ca[q, j, job.at] = cz[q, j]
 
+    def put(job, i, side):
+        src = (ca, cb)[side].at[job.q, i]
+        at = 1 - core if side else core
+        return pltpu.make_async_copy(src, gconv_hbm.at[job.layer, job.taps[i], at], oc_sem.at[job.q, i, side])
+
     def conv_cag(job):
         q = job.q
         for i, j in enumerate(job.taps):
@@ -595,13 +641,13 @@
                 slot, dev = job.ring(d)
                 rcopy(cz.at[q, i], ca.at[q, i, slot], cas.at[q, i, slot], cars.at[q, i, slot], dev).wait()
             rcopy(ca.at[q, i], cb.at[q, i], cbs.at[q, i], cbrs.at[q, i], other).start()
-            gconv_ref[job.layer, j, core] = ca[q, i]
+            put(job, i, 0).start()
 
     def conv_end(job):
         q = job.q
         for i, j in enumerate(job.taps):
             rcopy(ca.at[q, i], cb.at[q, i], cbs.at[q, i], cbrs.at[q, i], other).wait()
-            gconv_ref[job.layer, j, 1 - core] = cb[q, i]
+            put(job, i, 1).start()
         for i in range(job.owners):
             @pl.when(job.me != i)
             def _(i=i):
@@ -687,32 +733,33 @@
 
         def early(l=l, span=span):
             if l == 0:
-                conv_ag(jobs[0])
+                conv_rs(jobs[0])
                 _, inv, gain, _ = norms[0]
 
                 def body(o, _):
                     v = g[pl.ds(o, CH), :] + gain * inv * dpre[pl.ds(o, CH), :]
                     asend[o // Q, pl.ds(lax.rem(o, Q), CH), :] = v.astype(BF16)
                 chunks(body)
+                conv_rs(jobs[2])
+                conv_rs(jobs[1])
                 a2a(3, asend, arecv, "start")
                 arecv[x] = asend[x]
-                conv_rs(jobs[2])
-                conv_rs(jobs[1])
             else:
                 conv_start(1, span, actTs[1], (0, 1, 2))
                 vmid()
-                conv_x(jobs[0])
 
         def late(l=l):
             if l == 1:
+                conv_x(jobs[0])
                 ystart(4)
                 ystart(5)
                 vend()
-                conv_rs(jobs[0])
+                bias_own()
             else:
-                conv_xag(jobs[0])
                 conv_ag(jobs[2])
                 conv_ag(jobs[1])
+                conv_ag(jobs[0])
+                finish_head()
 
         s = sync(5 - l, value, False, early, late)
         report(l, s)
@@ -723,19 +770,27 @@
     def finish(o, _):
         xh = (seq_ref[pl.ds(o, CH), :].astype(F32) - mean) * inv
         part = blocked(arecv)(o)
-        gin_ref[pl.ds(o, CH), :] = part - gain * inv * (s[0:1] * (1.0 / n) + xh * (s[1:2] * (1.0 / n)))
+        g[pl.ds(o, CH), :] = part - gain * inv * (s[0:1] * (1.0 / n) + xh * (s[1:2] * (1.0 / n)))
     chunks(finish)
+    put_in = pltpu.make_async_copy(g, gin_hbm, out_sem.at[0])
+    put_in.start()
     conv_xag(jobs[2])
     conv_xag(jobs[1])
-    finish_head()
-    conv_cag(jobs[0])
+    conv_xag(jobs[0])
     bias_end()
+    collect_head()
     conv_cag(jobs[2])
     conv_cag(jobs[1])
-    conv_end(jobs[0])
-    collect_head()
+    conv_cag(jobs[0])
     conv_end(jobs[2])
     conv_end(jobs[1])
+    conv_end(jobs[0])
+    put_in.wait()
+    pltpu.make_async_copy(ghead_ref, ghead_hbm, out_sem.at[1]).wait()
+    for job in jobs:
+        for i in range(len(job.taps)):
+            put(job, i, 0).wait()
+            put(job, i, 1).wait()
 
 
 def emit(gin, ggain, gshift, ghead, gbias, gconv, *rest):
@@ -774,9 +829,10 @@
             sds((R, C), F32), sds((3, C), F32), sds((3, C), F32), sds((C // 16, tracks), F32), sds((tracks,), F32),
             sds((2, 3, 2, 4, 3, 16, C), BF16),
         ),
-        in_specs=[vmem, vmem, vmem, vmem, hbm, hbm, hbm],
-        out_specs=(vmem,) * 6,
+        in_specs=[hbm] * 7,
+        out_specs=(hbm, vmem, vmem, hbm, vmem, hbm),
         scratch_shapes=[
+            V((R, C), BF16), V((3, C), F32), V((3, C), F32), V((tracks,), F32), V((C // 16, tracks), F32),
             V((2, 3, C, C), BF16), V((tracks, C), BF16), V((256, C), BF16), V((C, W7), BF16),
             V((tracks, R), jnp.int32), V((256, R), jnp.int32), V((W7, Q), F32), V((48, Q), F32),
             V((4, Q, C), BF16), V((R, C), F32), V((4, Q, C), F32), V((4, Q, C), F32),
@@ -785,17 +841,17 @@
             V((C, R), F32), V((4, Q, C), BF16), V((4, Q, C), BF16),
             V((R, C), F32), V((R, C), F32), V((R + 2 * PAD, C), BF16), V((R, C), F32), V((R, C), F32),
             V((4, Q, C), BF16),
-            V((6, 8, 2, C), F32), V((6, 16, 2, C), F32), V((1, 8, 8, TW), F32), V((1, 16, 8, TW), F32),
+            V((6, 8, 2, C), F32), V((6, 16, 2, C), F32), V((1, 8, 8, TW), F32), V((8, 1, TW), F32), V((16, 1, TW), F32), V((8, 1, TW), F32),
             V((T7, 192, TW), BF16), V((T7, 192, TW), BF16), V((2, 192, TW), F32),
             V((T7, 4, 48, TW), BF16), V((T7, 4, 48, TW), BF16), V((T7, 2, 24, TW), BF16), V((16, 24, TW), BF16), V((T7, 24, TW), BF16),
             V((4, 4, 48, TW), BF16), V((4, 48, TW), BF16), V((4, 48, TW), BF16),
             V((3, C, C), F32), V((2, 3, C // 2, C), BF16), V((2, 3, C // 2, C), BF16), V((3, 3, 4, 48, C), BF16),
             V((3, 3, 4, 48, C), BF16), V((3, 9, 16, C), BF16), V((3, 16, 16, C), BF16), V((3, 3, 3, 16, C), BF16),
             V((3, 3, 4, 3, 16, C), BF16), V((3, 3, 4, 3, 16, C), BF16),
-            D((6,)), D((8,)), D((16,)), D((6, 8)), D((6, 16)), D((4, 4)), D((4, 4)),
-            D((8,)), D((16,)), D((1, 8)), D((1, 16)), D((T7,)), D((T7,)), D((T7, 4)), D((T7, 4)), D((T7, 2)), D((16,)),
+            D((10,)), D((8,)), D((16,)), D((6, 8)), D((6, 16)), D((4, 4)), D((4, 4)),
+            D((8,)), D((16,)), D((1, 8)), D((8,)), D((8,)), D((16,)), D((T7,)), D((T7,)), D((T7, 4)), D((T7, 4)), D((T7, 2)), D((16,)),
             D((8,)), D((T7,)), D((4,)), D((4,)), D((4,)), D((4,)),
-            D((2, 3)), D((2, 3)), D((3, 3, 4)), D((3, 3, 4)), D((3, 9)), D((3, 16)), D((3, 16)), D((3, 9)), D((3, 3, 4)), D((3, 3, 4)),
+            D((2,)), D((3, 3, 2)), D((2, 3)), D((2, 3)), D((3, 3, 4)), D((3, 3, 4)), D((3, 9)), D((3, 16)), D((3, 16)), D((3, 9)), D((3, 3, 4)), D((3, 3, 4)),
             D((3, 3)), D((3, 3)),
         ],
         compiler_params=pltpu.CompilerParams(

time: 121 us -> 118 us (0.975)
  Pallas kernels: 119 us -> 116 us
    pallas_call x1, Pallas kernels: 116 us -> 112 us  [on_device(): pl.pallas_call(kernel, out_shape=(sds((R, C), F32), sds((3, C), F32), sds...]
where the time goes in v4:
time: 118 us; the launch traced here: 117 us
  Pallas kernels  116 us (98%)
    pallas_call x1, Pallas kernels, on_device(): pl.pallas_call(kernel, out_shape=(sds((R, C), F32), sds((3, C), F32), sds...  112 us
    pallas_call x1, Pallas kernels, on_device(): pl.pallas_call(emit, out_shape=(sds((R, C), F32), sds((6, C, C), F32), sd...  3.41 us

profile of v4, /device:TPU:0, one launch (start us, length us, event | category | flops | bytes accessed | tf_op | source)
XLA Modules:
  0.0 116.7 jit_solution(15994889464343721036)
XLA Ops:
  0.6 112.5 %whole.1 = (f32[512,384]{1,0:T(8,128)}, f32[3,384]{1,0:T(4,128)}, f32[3,384]{1,0:T(4,128)}, f32[24,5313]{1,0:T(8,128)}, f32[5313]{0:T(1024)}, /*index=5*/bf16[2,3,2,4,3,16,384]{6,5,4,3,2,1,0:T(8,128)(2,1)}) custom-call(bf16[512,384]{1,0:T(8,128)(2,1)} %bitcast.9, f32[3,384]{1,0:T(4,128)} %gain_hbm.1, f32[3,384]{1,0:T(4,128)} %shift_hbm.1, f32[5313]{0:T(1024)} %hb_hbm.1, ...), custom_call_target="tpu_custom_call" | custom-call | tf_op jit(solution)/shard_map/whole/pallas_call | solution.py:826
  113.1 3.4 %emit.1 = (f32[512,384]{1,0:T(8,128)}, f32[6,384,384]{2,1,0:T(8,128)}, f32[3,384]{1,0:T(4,128)}, f32[3,384]{1,0:T(4,128)}, f32[24,5313]{1,0:T(8,128)}, /*index=5*/f32[5313]{0:T(1024)}) custom-call(f32[512,384]{1,0:T(8,128)} %get-tuple-element.18.gin, f32[3,384]{1,0:T(4,128)} %get-tuple-element.19.ggain, f32[3,384]{1,0:T(4,128)} %get-tuple-element.20.gshift, ...), custom_call_target="tpu_custom_call" | custom-call | tf_op jit(solution)/shard_map/emit/pallas_call | solution.py:862

commit v5 on v4

--- a/solution.py
+++ b/solution.py
@@ -545,8 +545,6 @@
         def _():
             xstart(full)
 
-    chip(5, 0)
-
     class Job:
         def __init__(self, number, layer, taps, at, ring, me, peer, dev):
             self.q, self.layer, self.taps, self.at, self.ring = number, layer, taps, at, ring
@@ -697,6 +695,7 @@
         a2a(2, dps, dpq, "start")
         dpq[x] = dps[x]
         xstart(4)
+        chip(5, 0)
         xstart(5)
 
     def fill32():

time: 118 us -> 118 us (level)
  no operation moved by 1% of the time
where the time goes in v5:
time: 118 us; the launch traced here: 117 us
  Pallas kernels  116 us (98%)
    pallas_call x1, Pallas kernels, on_device(): pl.pallas_call(kernel, out_shape=(sds((R, C), F32), sds((3, C), F32), sds...  112 us
    pallas_call x1, Pallas kernels, on_device(): pl.pallas_call(emit, out_shape=(sds((R, C), F32), sds((6, C, C), F32), sd...  3.41 us

profile of v5, /device:TPU:0, one launch (start us, length us, event | category | flops | bytes accessed | tf_op | source)
XLA Modules:
  0.0 116.6 jit_solution(489527937534646593)
XLA Ops:
  0.6 112.4 %whole.1 = (f32[512,384]{1,0:T(8,128)}, f32[3,384]{1,0:T(4,128)}, f32[3,384]{1,0:T(4,128)}, f32[24,5313]{1,0:T(8,128)}, f32[5313]{0:T(1024)}, /*index=5*/bf16[2,3,2,4,3,16,384]{6,5,4,3,2,1,0:T(8,128)(2,1)}) custom-call(bf16[512,384]{1,0:T(8,128)(2,1)} %bitcast.9, f32[3,384]{1,0:T(4,128)} %gain_hbm.1, f32[3,384]{1,0:T(4,128)} %shift_hbm.1, f32[5313]{0:T(1024)} %hb_hbm.1, ...), custom_call_target="tpu_custom_call" | custom-call | tf_op jit(solution)/shard_map/whole/pallas_call | solution.py:825
  113.1 3.4 %emit.1 = (f32[512,384]{1,0:T(8,128)}, f32[6,384,384]{2,1,0:T(8,128)}, f32[3,384]{1,0:T(4,128)}, f32[3,384]{1,0:T(4,128)}, f32[24,5313]{1,0:T(8,128)}, /*index=5*/f32[5313]{0:T(1024)}) custom-call(f32[512,384]{1,0:T(8,128)} %get-tuple-element.18.gin, f32[3,384]{1,0:T(4,128)} %get-tuple-element.19.ggain, f32[3,384]{1,0:T(4,128)} %get-tuple-element.20.gshift, ...), custom_call_target="tpu_custom_call" | custom-call | tf_op jit(solution)/shard_map/emit/pallas_call | solution.py:861
